TPU v7x, 32 devices: a whole 2x2x4 slice. The times are simulated.
32 devices in a mesh: head: 4 (over x, core), seq: 8 (over z, y).
Axes of the slice: x: 2, y: 2, z: 4, core: 2. Of those that a mesh axis runs over, the one named last changes fastest.
Arguments:
- queries: bfloat16 [2048, 4096], P('seq', 'head'), may hold values from -160 to 160
- encodings: bfloat16 [24, 128, 1024], P('seq', None, 'head'), may hold values from -6 to 6
- kv_weight: bfloat16 [2, 1024, 4096], P(None, None, 'head'), may hold values from -0.1875 to 0.1875
- grad_out: bfloat16 [2048, 4096], P('seq', 'head'), may hold values from -6 to 6
- neighbour_owner: int32 [32, 2], replicated, may hold values from 0 to 7, all different within a row; in each aligned block of 4 rows (0 to 3, 4 to 7, ...) at most 2 rows name the same one
- neighbour_slot: int32 [32, 2], replicated, may hold values from 0 to 2
Outputs:
- attended: bfloat16 [2048, 4096], P('seq', 'head')
- query_grad: bfloat16 [32, 64, 4096], P('seq', 'head')
- encoding_grad: bfloat16 [24, 128, 1024], P('seq', None, 'head')
Inputs may be any that keep to these rules, and one draw needn't show every extreme that they name: `neighbour_owner`: the 2 owners of one span differ. Among the 4 spans of one index of seq (aligned blocks of rows), no owner is named more than 2 times, and in every draw some owner is named exactly 2 times.
All inputs are finite; a program needn't handle non-finite values.
Results may differ from a plain program's by a relative error of at most 0.019.
The roundings to bfloat16 on the way count: a program that leaves them out, or rounds other values in their place, can miss the bound.
Values may be sent and summed in bfloat16 or wider, within the bound.
A program may use at most 64 MiB of HBM per device.

v0:
```python
import jax
import jax.numpy as jnp
from jax import lax
from jax.sharding import PartitionSpec as P

HEAD_DIM = 128
SPAN = 64
NEIGHBOURS = 2
NEIGHBOUR_LEN = 128


def passed_along(array, axis, by):
    count = lax.axis_size(axis)
    pairs = [(i, i + by) for i in range(count) if 0 <= i + by < count]
    return lax.ppermute(array, axis, pairs)


def per_device(queries, encodings, kv_weight, grad_out, neighbour_owner, neighbour_slot):
    seq_count = lax.axis_size("seq")
    seq_index = lax.axis_index("seq")
    scale = HEAD_DIM ** (-0.5)
    token_rows = queries.shape[0]
    local_width = queries.shape[1]
    local_heads = local_width // HEAD_DIM
    spans_local = token_rows // SPAN
    groups = spans_local + 1
    requests = spans_local * NEIGHBOURS
    capacity = max(2, (requests + seq_count - 1) // seq_count)
    tile_rows = encodings.shape[0]
    slice_width = encodings.shape[2]
    window = NEIGHBOURS * NEIGHBOUR_LEN
    owners_all = neighbour_owner.reshape(seq_count, requests)
    slots_all = neighbour_slot.reshape(seq_count, requests)
    order = jnp.arange(requests)
    earlier = order[:, None] > order[None, :]
    same_owner = owners_all[:, :, None] == owners_all[:, None, :]
    ranks_all = jnp.sum((same_owner & earlier[None]).astype(jnp.int32), axis=2)
    my_owner = lax.dynamic_index_in_dim(owners_all, seq_index, 0, keepdims=False)
    my_rank = lax.dynamic_index_in_dim(ranks_all, seq_index, 0, keepdims=False)
    slot_place = my_owner * capacity + my_rank
    matched = (owners_all == seq_index)[:, :, None] & (
        ranks_all[:, :, None] == jnp.arange(capacity)[None, None, :]
    )
    matched = matched.astype(jnp.int32)
    chosen = jnp.sum(matched * slots_all[:, :, None], axis=1).reshape(-1)
    filled = jnp.sum(matched, axis=1).reshape(-1)
    target = jnp.where(filled > 0, chosen, tile_rows)
    outgoing = jnp.where(filled[:, None, None] > 0, encodings[chosen], jnp.zeros((), jnp.bfloat16))
    outgoing = outgoing.reshape(seq_count, capacity, NEIGHBOUR_LEN, slice_width)
    incoming = lax.all_to_all(outgoing, "seq", split_axis=0, concat_axis=0, tiled=True)
    picked = incoming.reshape(seq_count * capacity, NEIGHBOUR_LEN, slice_width)[slot_place]
    features = lax.all_gather(picked, "head", axis=2, tiled=True)
    projected = jnp.einsum(
        "rle,ced->crld", features, kv_weight, preferred_element_type=jnp.float32
    ).astype(jnp.bfloat16)
    by_span = projected.reshape(2, spans_local, window, local_width)
    carried = passed_along(by_span[:, -1], "seq", 1)
    extended = jnp.concatenate([carried[:, None], by_span], axis=1)
    extended = extended.reshape(2, groups, window, local_heads, HEAD_DIM)
    key_block = extended[0]
    value_block = extended[1]

    def padded_groups(rows):
        padded = jnp.concatenate(
            [
                jnp.zeros((1, local_width), rows.dtype),
                rows,
                jnp.zeros((SPAN - 1, local_width), rows.dtype),
            ],
            0,
        )
        return padded.reshape(groups, SPAN, local_heads, HEAD_DIM)

    query_pad = padded_groups(queries)
    grad_pad = padded_groups(grad_out)
    scores = (
        jnp.einsum("gqhd,gkhd->ghqk", query_pad, key_block, preferred_element_type=jnp.float32)
        * scale
    )
    top = jnp.max(scores, axis=-1, keepdims=True)
    expo = jnp.exp(scores - top)
    probs = expo / jnp.sum(expo, axis=-1, keepdims=True)
    probs_half = probs.astype(jnp.bfloat16)
    output = jnp.einsum(
        "ghqk,gkhd->gqhd", probs_half, value_block, preferred_element_type=jnp.float32
    )
    attended = output.reshape(groups * SPAN, local_width)[1 : 1 + token_rows].astype(jnp.bfloat16)
    dprob = jnp.einsum("gqhd,gkhd->ghqk", grad_pad, value_block, preferred_element_type=jnp.float32)
    delta = jnp.sum(probs * dprob, axis=-1, keepdims=True)
    dscore = (probs * (dprob - delta)).astype(jnp.bfloat16)
    qgrad = (
        jnp.einsum("ghqk,gkhd->gqhd", dscore, key_block, preferred_element_type=jnp.float32) * scale
    )
    kgrad = (
        jnp.einsum("ghqk,gqhd->gkhd", dscore, query_pad, preferred_element_type=jnp.float32) * scale
    )
    vgrad = jnp.einsum("ghqk,gqhd->gkhd", probs_half, grad_pad, preferred_element_type=jnp.float32)
    qgrad_rows = qgrad.reshape(groups * SPAN, local_width)[1 : 1 + token_rows].astype(jnp.bfloat16)
    qgrad_rows = qgrad_rows.reshape(spans_local, SPAN, local_width)
    query_grad = lax.all_to_all(qgrad_rows, "head", split_axis=1, concat_axis=2, tiled=True)
    kv_grad = jnp.stack([kgrad, vgrad], 0).reshape(2, groups, window, local_width)
    returned = passed_along(kv_grad[:, 0], "seq", -1)
    own_grad = kv_grad[:, 1:].at[:, -1].add(returned)
    grad_half = own_grad.astype(jnp.bfloat16).reshape(2, requests, NEIGHBOUR_LEN, local_width)
    flat_half = grad_half.reshape(2, requests * NEIGHBOUR_LEN, local_width)
    term = jnp.einsum("cnd,ced->ne", flat_half, kv_weight, preferred_element_type=jnp.float32)
    term = term.reshape(requests, NEIGHBOUR_LEN, -1)
    request_grad = lax.psum_scatter(term, "head", scatter_dimension=2, tiled=True)
    outgoing_grad = jnp.zeros((seq_count * capacity, NEIGHBOUR_LEN, slice_width), jnp.float32)
    outgoing_grad = outgoing_grad.at[slot_place].set(request_grad)
    outgoing_grad = outgoing_grad.reshape(seq_count, capacity, NEIGHBOUR_LEN, slice_width)
    incoming_grad = lax.all_to_all(outgoing_grad, "seq", split_axis=0, concat_axis=0, tiled=True)
    summed = jnp.zeros((tile_rows + 1, NEIGHBOUR_LEN, slice_width), jnp.float32)
    summed = summed.at[target].add(
        incoming_grad.reshape(seq_count * capacity, NEIGHBOUR_LEN, slice_width)
    )
    tile_grad = summed[:tile_rows]
    return (attended, query_grad, tile_grad.astype(jnp.bfloat16))


def solution(mesh):
    in_specs = (
        P("seq", "head"),
        P("seq", None, "head"),
        P(None, None, "head"),
        P("seq", "head"),
        P(),
        P(),
    )
    out_specs = (P("seq", "head"), P("seq", "head", None), P("seq", None, "head"))
    return jax.shard_map(
        per_device, mesh=mesh, in_specs=in_specs, out_specs=out_specs, check_vma=False
    )
```

profile of v0, /device:TPU:0, one launch (start us, length us, event | category | flops | bytes accessed | tf_op | source)
XLA Modules:
  0.0 320.8 jit_solution(1670462678393541136)
XLA Ops:
  11.5 7.3 %all-to-all-start = ((bf16[8,2,128,256]{3,2,1,0:T(8,128)(2,1)}), bf16[8,2,128,256]{3,2,1,0:T(8,128)(2,1)S(1)}, u32[]{:S(2)}, u32[]{:S(2)}) async-start(bf16[8,2,128,256]{3,2,1,0:T(8,128)(2,1)} %broadcast_select_fusion), calls=%async_computation | async-start | bytes 2097152 | tf_op jit(solution)/shard_map/all_to_all | solution.py:50
  18.9 25.7 %all-to-all-done = bf16[8,2,128,256]{3,2,1,0:T(8,128)(2,1)S(1)} async-done(((bf16[8,2,128,256]{3,2,1,0:T(8,128)(2,1)}), bf16[8,2,128,256]{3,2,1,0:T(8,128)(2,1)S(1)}, u32[]{:S(2)}, u32[]{:S(2)}) %all-to-all-start) | async-done | bytes 1048608 | tf_op jit(solution)/shard_map/all_to_all | solution.py:50
  46.0 22.0 %all-gather.3.cloned.1.call-done = bf16[8,128,1024]{2,1,0:T(8,128)(2,1)} async-done(((bf16[8,128,256]{2,1,0:T(8,128)(2,1)}), bf16[8,128,1024]{2,1,0:T(8,128)(2,1)}) %all-gather.3.cloned.1.call-update) | async-done | bytes 2097168 | tf_op jit(solution)/shard_map/all_gather | solution.py:52
  67.9 7.3 %convert_bitcast_fusion = bf16[2,8,128,1024]{3,2,0,1:T(8,128)(2,1)S(1)} fusion(bf16[2,1024,1024]{2,1,0:T(8,128)(2,1)} %param.10, bf16[8,128,1024]{2,1,0:T(8,128)(2,1)} %all-gather.3.cloned.1.call-done), kind=kOutput, calls=%fused_computation.16 | convolution fusion | flops 4297064448 | bytes 10485760 | tf_op jit(solution)/shard_map/rle,ced->crld/dot_general | solution.py:53
  76.0 3.6 %collective-permute-start = (bf16[2,256,1024]{2,1,0:T(8,128)(2,1)S(1)}, bf16[2,256,1024]{2,1,0:T(8,128)(2,1)S(1)}, u32[]{:S(2)}, u32[]{:S(2)}) collective-permute-start(bf16[2,256,1024]{2,1,0:T(8,128)(2,1)S(1)} %slice_bitcast_fusion), channel_id=1, source_target_pairs={{0,1},{1,2},{2,3},{3,4},{4,5},{5,6},{6,7},{8,9},{9,10},{10,11},{11... | collective-permute-start | bytes 3145736 | tf_op jit(solution)/shard_map/ppermute | solution.py:15
  81.4 20.8 %collective-permute-done = bf16[2,256,1024]{2,1,0:T(8,128)(2,1)S(1)} collective-permute-done((bf16[2,256,1024]{2,1,0:T(8,128)(2,1)S(1)}, bf16[2,256,1024]{2,1,0:T(8,128)(2,1)S(1)}, u32[]{:S(2)}, u32[]{:S(2)}) %collective-permute-start) | collective-permute-done | bytes 1048608 | tf_op jit(solution)/shard_map/ppermute | solution.py:15
  102.2 2.6 pad_maximum_fusion
  104.8 3.0 copy.86
  107.8 5.0 %copy.85 = bf16[1,5,256,1024]{2,3,1,0:T(8,128)(2,1)} copy(bf16[1,5,256,1024]{3,2,1,0:T(8,128)(2,1)} %get-tuple-element.18) | data formatting | bytes 5242880 | tf_op jit(solution)/shard_map/slice | solution.py:61
  113.2 7.0 %fusion.49 = (f32[5,8,64]{2,1,0:T(8,128)S(1)}, f32[5,8,64,256]{3,2,1,0:T(8,128)S(1)}) fusion(f32[5,8,64,256]{3,2,1,0:T(8,128)S(1)} %fusion.32), kind=kOutput, calls=%fused_computation.77 | output fusion | flops 2621695 | bytes 5253120 | tf_op jit(solution)/shard_map/sub | solution.py:81
  120.2 10.1 %fusion.25 = f32[5,8,128,256]{3,2,1,0:T(8,128)} fusion(bf16[5,64,8,128]{3,2,1,0:T(8,128)(2,1)} %bitcast.121, f32[5,8,64]{2,1,0:T(8,128)S(1)} %get-tuple-element.23, f32[5,8,64,256]{3,2,1,0:T(8,128)} %copy-done.6), kind=kOutput, calls=%fused_computation.46 | convolution fusion | flops 171051776 | bytes 8529920 | tf_op jit(solution)/shard_map/ghqk,gqhd->gkhd/dot_general | solution.py:97
  130.3 6.0 %copy.102 = f32[1,5,256,1024]{3,2,0,1:T(8,128)} copy(f32[1,5,256,1024]{2,3,1,0:T(8,128)} %bitcast.108) | data formatting | bytes 10485760 | tf_op jit(solution)/shard_map/stack | solution.py:101
  136.3 3.0 multiply_reduce_fusion
  140.3 3.3 %broadcast_multiply_fusion = f32[5,8,128,256]{3,2,1,0:T(8,128)} fusion(bf16[5,8,64,256]{3,2,1,0:T(8,128)(2,1)S(1)} %multiply_convert_fusion, bf16[5,64,8,128]{3,2,1,0:T(8,128)(2,1)S(1)} %bitcast.107), kind=kOutput, calls=%fused_computation.19 | convolution fusion | flops 169082880 | bytes 7208960 | tf_op jit(solution)/shard_map/ghqk,gqhd->gkhd/dot_general | solution.py:95
  143.5 6.1 %copy.101 = f32[1,5,256,1024]{3,2,0,1:T(8,128)} copy(f32[1,5,256,1024]{2,3,1,0:T(8,128)} %bitcast.104) | data formatting | bytes 10485760 | tf_op jit(solution)/shard_map/stack | solution.py:101
  155.2 46.3 %collective-permute-done.1 = f32[2,256,1024]{2,1,0:T(8,128)S(1)} collective-permute-done((f32[2,256,1024]{2,1,0:T(8,128)S(1)}, f32[2,256,1024]{2,1,0:T(8,128)S(1)}, u32[]{:S(2)}, u32[]{:S(2)}) %collective-permute-start.1) | collective-permute-done | bytes 2097184 | tf_op jit(solution)/shard_map/ppermute | solution.py:15
  201.8 6.1 %fusion.12 = f32[8,128,1024]{2,1,0:T(8,128)} fusion(bf16[8,128,2,1024]{3,1,0,2:T(8,128)(2,1)S(1)} %bitcast.109, bf16[2,1024,1024]{2,1,0:T(8,128)(2,1)S(1)} %copy-done.10), kind=kOutput, calls=%fused_computation.25 | convolution fusion | flops 4294967296 | bytes 12582912 | tf_op jit(solution)/shard_map/cnd,ced->ne/dot_general | solution.py:106
  209.6 2.3 fusion.23
  213.9 3.5 %all-to-all-start.1 = ((bf16[4,64,1024]{2,0,1:T(4,128)(2,1)}), bf16[4,64,1024]{2,0,1:T(4,128)(2,1)S(1)}, u32[]{:S(2)}, u32[]{:S(2)}) async-start(bf16[4,64,1024]{2,0,1:T(4,128)(2,1)} %copy.95), calls=%async_computation.1 | async-start | bytes 1048576 | tf_op jit(solution)/shard_map/all_to_all | solution.py:100
  217.4 35.4 %reduce-scatter.2.cloned.1.call-done = f32[8,128,256]{2,1,0:T(8,128)} async-done(((f32[8,128,1024]{2,1,0:T(8,128)}), f32[8,128,256]{2,1,0:T(8,128)}) %reduce-scatter.2.cloned.1.call-update) | async-done | bytes 1048592 | tf_op jit(solution)/shard_map/reduce_scatter | solution.py:108
  254.3 2.9 scatter_fusion
  257.2 5.5 %all-to-all-start.2 = ((f32[8,2,128,256]{3,2,1,0:T(8,128)}), f32[8,2,128,256]{3,2,1,0:T(8,128)S(1)}, u32[]{:S(2)}, u32[]{:S(2)}) async-start(f32[8,2,128,256]{3,2,1,0:T(8,128)} %bitcast.32), calls=%async_computation.3 | async-start | bytes 4194304 | tf_op jit(solution)/shard_map/all_to_all | solution.py:112
  262.7 7.9 %fusion.24 = bf16[5,64,8,128]{3,1,2,0:T(8,128)(2,1)S(1)} fusion(bf16[5,256,8,128]{1,3,2,0:T(8,128)(2,1)} %bitcast.112, f32[5,8,64]{2,1,0:T(8,128)S(1)} %get-tuple-element.23, f32[5,8,64,256]{3,2,1,0:T(8,128)} %copy-done.6), kind=kOutput, calls=%fused_computation.39 | convolution fusion | flops 171379456 | bytes 5908480 | tf_op jit(solution)/shard_map/ghqk,gkhd->gqhd/dot_general | solution.py:84
  273.1 37.9 %all-to-all-done.2 = f32[8,2,128,256]{3,2,1,0:T(8,128)S(1)} async-done(((f32[8,2,128,256]{3,2,1,0:T(8,128)}), f32[8,2,128,256]{3,2,1,0:T(8,128)S(1)}, u32[]{:S(2)}, u32[]{:S(2)}) %all-to-all-start.2) | async-done | bytes 2097184 | tf_op jit(solution)/shard_map/all_to_all | solution.py:112
  (80 shorter events, 26.1 us)
Async XLA Ops:
  7.2 2.6 copy-start
  11.5 33.0 %all-to-all-start = ((bf16[8,2,128,256]{3,2,1,0:T(8,128)(2,1)}), bf16[8,2,128,256]{3,2,1,0:T(8,128)(2,1)S(1)}, u32[]{:S(2)}, u32[]{:S(2)}) async-start(bf16[8,2,128,256]{3,2,1,0:T(8,128)(2,1)} %broadcast_select_fusion), calls=%async_computation | async-start | bytes 2097152 | tf_op jit(solution)/shard_map/all_to_all | solution.py:50
  18.8 49.2 %all-gather.3.cloned.1.call-start = ((), (), s32[]{:S(2)}) async-start(), calls=%async_computation.5 | async-start | bytes 2621440 | tf_op jit(solution)/shard_map/all_gather | solution.py:52
  45.9 206.8 %reduce-scatter.2.cloned.1.call-start = ((), (), s32[]{:S(2)}) async-start(), calls=%async_computation.4 | async-start | bytes 5242880 | tf_op jit(solution)/shard_map/reduce_scatter | solution.py:108
  75.3 4.4 %copy-start.8 = (bf16[256,1024]{1,0:T(8,128)(2,1)S(1)}, bf16[256,1024]{1,0:T(8,128)(2,1)}, u32[]{:S(2)}) copy-start(bf16[256,1024]{1,0:T(8,128)(2,1)} %param.11) | copy-start | bytes 1572868
  75.3 4.4 %copy-start.9 = (bf16[256,1024]{1,0:T(8,128)(2,1)S(1)}, bf16[256,1024]{1,0:T(8,128)(2,1)}, u32[]{:S(2)}) copy-start(bf16[256,1024]{1,0:T(8,128)(2,1)} %param.8) | copy-start | bytes 1572868
  76.0 26.2 %collective-permute-start = (bf16[2,256,1024]{2,1,0:T(8,128)(2,1)S(1)}, bf16[2,256,1024]{2,1,0:T(8,128)(2,1)S(1)}, u32[]{:S(2)}, u32[]{:S(2)}) collective-permute-start(bf16[2,256,1024]{2,1,0:T(8,128)(2,1)S(1)} %slice_bitcast_fusion), channel_id=1, source_target_pairs={{0,1},{1,2},{2,3},{3,4},{4,5},{5,6},{6,7},{8,9},{9,10},{10,11},{11... | collective-permute-start | bytes 3145736 | tf_op jit(solution)/shard_map/ppermute | solution.py:15
  107.8 5.0 %copy-start.3 = (bf16[1,5,256,1024]{2,3,1,0:T(8,128)(2,1)}, bf16[1,5,256,1024]{2,3,1,0:T(8,128)(2,1)S(1)}, u32[]{:S(2)}) copy-start(bf16[1,5,256,1024]{2,3,1,0:T(8,128)(2,1)S(1)} %copy.86) | copy-start | bytes 7864324
  113.2 7.0 %copy-start.6 = (f32[5,8,64,256]{3,2,1,0:T(8,128)}, f32[5,8,64,256]{3,2,1,0:T(8,128)S(1)}, u32[]{:S(2)}) copy-start(f32[5,8,64,256]{3,2,1,0:T(8,128)S(1)} %fusion.32) | copy-start | bytes 7864324
  140.3 3.3 %copy-start.5 = (bf16[5,8,64,256]{3,2,1,0:T(8,128)(2,1)}, bf16[5,8,64,256]{3,2,1,0:T(8,128)(2,1)S(1)}, u32[]{:S(2)}) copy-start(bf16[5,8,64,256]{3,2,1,0:T(8,128)(2,1)S(1)} %multiply_convert_fusion) | copy-start | bytes 3932164
  143.5 9.7 %slice-start = ((s8[5242880]{0:T(1024)(128)(4,1)}), s8[1048576]{0:T(1024)(128)(4,1)S(1)}, s32[]{:S(2)}) async-start(s8[5242880]{0:T(1024)(128)(4,1)} %bitcast.98), calls=%async_computation.6 | async-start | bytes 2097152
  149.6 3.6 %slice-start.1 = ((s8[5242880]{0:T(1024)(128)(4,1)}), s8[4194304]{0:T(1024)(128)(4,1)S(1)}, s32[]{:S(2)}) async-start(s8[5242880]{0:T(1024)(128)(4,1)} %bitcast.98), calls=%async_computation.7 | async-start | bytes 8388608
  149.6 4.4 %copy-start.2 = (f32[1,5,256,1024]{3,2,0,1:T(8,128)S(1)}, f32[1,5,256,1024]{3,2,0,1:T(8,128)}, u32[]{:S(2)}) copy-start(f32[1,5,256,1024]{3,2,0,1:T(8,128)} %copy.101) | copy-start | bytes 15728644
  151.5 50.0 %collective-permute-start.1 = (f32[2,256,1024]{2,1,0:T(8,128)S(1)}, f32[2,256,1024]{2,1,0:T(8,128)S(1)}, u32[]{:S(2)}, u32[]{:S(2)}) collective-permute-start(f32[2,256,1024]{2,1,0:T(8,128)S(1)} %fusion.19), channel_id=1, source_target_pairs={{1,0},{2,1},{3,2},{4,3},{5,4},{6,5},{7,6},{9,8},{10,9},{11,10},{12... | collective-permute-start | bytes 6291464 | tf_op jit(solution)/shard_map/ppermute | solution.py:15
  155.2 46.6 %copy-start.10 = (bf16[2,1024,1024]{2,1,0:T(8,128)(2,1)S(1)}, bf16[2,1024,1024]{2,1,0:T(8,128)(2,1)}, u32[]{:S(2)}) copy-start(bf16[2,1024,1024]{2,1,0:T(8,128)(2,1)} %param.10) | copy-start | bytes 12582916
  207.9 1.7 copy-start.4
  213.9 43.3 %all-to-all-start.1 = ((bf16[4,64,1024]{2,0,1:T(4,128)(2,1)}), bf16[4,64,1024]{2,0,1:T(4,128)(2,1)S(1)}, u32[]{:S(2)}, u32[]{:S(2)}) async-start(bf16[4,64,1024]{2,0,1:T(4,128)(2,1)} %copy.95), calls=%async_computation.1 | async-start | bytes 1048576 | tf_op jit(solution)/shard_map/all_to_all | solution.py:100
  252.8 1.6 copy-start.7
  257.2 53.8 %all-to-all-start.2 = ((f32[8,2,128,256]{3,2,1,0:T(8,128)}), f32[8,2,128,256]{3,2,1,0:T(8,128)S(1)}, u32[]{:S(2)}, u32[]{:S(2)}) async-start(f32[8,2,128,256]{3,2,1,0:T(8,128)} %bitcast.32), calls=%async_computation.3 | async-start | bytes 4194304 | tf_op jit(solution)/shard_map/all_to_all | solution.py:112
  311.0 2.9 copy-start.1
Sparse Core Ops, SparseCore 0:
  46.1 21.8 all-gather.2
  208.0 44.6 reduce-scatter.1
where the time goes:
time: 322 us; the launch traced here: 321 us
  waiting for transfers between devices  188 us (58%)
  matrix products  40.4 us (13%)
  local copies, waits for them, and re-layouts  38.5 us (12%)
  starting transfers between devices  21.8 us (7%)
  other arithmetic  17.8 us (6%)
  between operations  14.4 us (4%)
    ppermute x2, waiting for transfers between devices, passed_along(): return lax.ppermute(array, axis, pairs)  67 us
    all_to_all x1, waiting for transfers between devices, per_device(): lax.all_to_all(outgoing_grad, 'seq', split_axis=0, concat_axis=0, tiled=T...  37.9 us
    reduce_scatter x1, waiting for transfers between devices, per_device(): lax.psum_scatter(term, 'head', scatter_dimension=2, tiled=True)  35.4 us
    all_to_all x1, waiting for transfers between devices, per_device(): lax.all_to_all(outgoing, 'seq', split_axis=0, concat_axis=0, tiled=True)  25.7 us
    all_gather x1, waiting for transfers between devices, per_device(): features = lax.all_gather(picked, 'head', axis=2, tiled=True)  22 us
    another operation x2, local copies, waits for them, and re-layouts, per_device(): jnp.stack([kgrad, vgrad], 0).reshape(2, groups, window, local_width)  12.1 us
    dot_general x1, matrix products, per_device(): jnp.einsum('ghqk,gqhd->gkhd', probs_half, grad_pad, preferred_element_typ...  10.1 us
    dot_general x1, matrix products, per_device(): jnp.einsum('ghqk,gkhd->gqhd', probs_half, value_block, preferred_element_...  7.86 us
  transfers between devices with their start and end apart: 7, of which 6 were waited for; matrix products, arithmetic and copies ran while one was open for 7% of the time, Pallas kernels for 0%

commit v1 on v0

v1 whole, which is shorter than its diff:
```python
import functools

import jax
import jax.numpy as jnp
from jax import lax
from jax.experimental import pallas as pl
from jax.experimental.pallas import tpu as pltpu
from jax.sharding import PartitionSpec as P

HEAD_DIM = 128
SPAN = 64
NEIGHBOURS = 2
NEIGHBOUR_LEN = 128
WINDOW = NEIGHBOURS * NEIGHBOUR_LEN
SCALE = HEAD_DIM ** (-0.5)
F32 = jnp.float32
BF16 = jnp.bfloat16


def dot(a, b, da, db):
    return lax.dot_general(a, b, (((da,), (db,)), ((), ())), preferred_element_type=F32)


def group_body(feat_ref, weight_ref, query_ref, grad_ref, att_ref, qgrad_ref, term_ref, kv, kv_grad):
    parts, _, part = feat_ref.shape
    width = query_ref.shape[1]
    for c in range(2):
        total = None
        for j in range(parts):
            piece = dot(feat_ref[j], weight_ref[c, j * part : (j + 1) * part, :], 1, 0)
            total = piece if total is None else total + piece
        kv[c] = total.astype(BF16)
    for h in range(width // HEAD_DIM):
        cols = slice(h * HEAD_DIM, (h + 1) * HEAD_DIM)
        q = query_ref[:, cols]
        g = grad_ref[:, cols]
        k = kv[0, :, cols]
        v = kv[1, :, cols]
        scores = dot(q, k, 1, 1) * SCALE
        dprob = dot(g, v, 1, 1)
        expo = jnp.exp(scores - jnp.max(scores, axis=-1, keepdims=True))
        probs = expo / jnp.sum(expo, axis=-1, keepdims=True)
        half = probs.astype(BF16)
        delta = jnp.sum(probs * dprob, axis=-1, keepdims=True)
        dscore = (probs * (dprob - delta)).astype(BF16)
        att_ref[:, cols] = dot(half, v, 1, 0).astype(BF16)
        qgrad_ref[:, cols] = (dot(dscore, k, 1, 0) * SCALE).astype(BF16)
        kv_grad[0, :, cols] = (dot(dscore, q, 0, 0) * SCALE).astype(BF16)
        kv_grad[1, :, cols] = dot(half, g, 0, 0).astype(BF16)
    for j in range(parts):
        rows = slice(j * part, (j + 1) * part)
        term_ref[j] = dot(kv_grad[0], weight_ref[0, rows, :], 1, 1) + dot(
            kv_grad[1], weight_ref[1, rows, :], 1, 1
        )


def run_groups(features, kv_weight, query_rows, grad_rows):
    parts, rows, part = features.shape
    token_rows, width = query_rows.shape
    groups = token_rows // SPAN
    token_spec = pl.BlockSpec((SPAN, width), lambda i: (i, 0))
    return pl.pallas_call(
        group_body,
        grid=(groups,),
        in_specs=[
            pl.BlockSpec((parts, WINDOW, part), lambda i: (0, i, 0)),
            pl.BlockSpec(kv_weight.shape, lambda i: (0, 0, 0), pipeline_mode=pl.Buffered(1)),
            token_spec,
            token_spec,
        ],
        out_specs=[
            token_spec,
            token_spec,
            pl.BlockSpec((parts, WINDOW, part), lambda i: (0, i, 0)),
        ],
        out_shape=[
            jax.ShapeDtypeStruct((token_rows, width), BF16),
            jax.ShapeDtypeStruct((token_rows, width), BF16),
            jax.ShapeDtypeStruct((parts, rows, part), F32),
        ],
        scratch_shapes=[
            pltpu.VMEM((2, WINDOW, width), BF16),
            pltpu.VMEM((2, WINDOW, width), BF16),
        ],
        compiler_params=pltpu.CompilerParams(
            dimension_semantics=("arbitrary",), vmem_limit_bytes=40 << 20
        ),
    )(features, kv_weight, query_rows, grad_rows)


def per_device(queries, encodings, kv_weight, grad_out, neighbour_owner, neighbour_slot):
    seq_count = lax.axis_size("seq")
    seq_index = lax.axis_index("seq")
    token_rows, width = queries.shape
    requests = token_rows // SPAN * NEIGHBOURS
    tile_rows, _, part = encodings.shape
    forward = [(i, (i + 1) % seq_count) for i in range(seq_count)]
    backward = [((i + 1) % seq_count, i) for i in range(seq_count)]

    tile = neighbour_owner * tile_rows + neighbour_slot
    tile = jnp.roll(tile, 1, axis=0).reshape(seq_count, requests)
    tile = lax.dynamic_index_in_dim(tile, seq_index, 0, keepdims=False)

    stored = lax.all_gather(encodings, "seq", axis=0, tiled=True)
    picked = stored[tile].reshape(requests * NEIGHBOUR_LEN, part)
    features = lax.all_gather(picked, "head", axis=0, tiled=False)

    edge = jnp.stack([queries[-1:], grad_out[-1:]], 0)
    edge = lax.ppermute(edge, "seq", forward)
    row = lax.broadcasted_iota(jnp.int32, (token_rows, 1), 0)
    unattending = (seq_index == 0) & (row >= 1) & (row < SPAN)
    zero = jnp.zeros((), BF16)

    def shifted(rows, first):
        rows = jnp.concatenate([first, rows[:-1]], 0)
        return jnp.where(unattending, zero, rows)

    query_rows = shifted(queries, edge[0])
    grad_rows = shifted(grad_out, edge[1])
    att, qgrad, term = run_groups(features, kv_weight, query_rows, grad_rows)

    att = jnp.where(unattending, zero, att)
    last = lax.ppermute(jnp.stack([att[:1], qgrad[:1]], 0), "seq", backward)
    attended = jnp.concatenate([att[1:], last[0]], 0)
    qgrad = jnp.concatenate([qgrad[1:], last[1]], 0).reshape(-1, SPAN, width)
    query_grad = lax.all_to_all(qgrad, "head", split_axis=1, concat_axis=2, tiled=True)

    mine = lax.psum_scatter(term, "head", scatter_dimension=0, tiled=True)
    mine = mine.reshape(requests, NEIGHBOUR_LEN, part)
    tiles = jnp.zeros((seq_count * tile_rows, NEIGHBOUR_LEN, part), F32).at[tile].add(mine)
    total = lax.psum_scatter(tiles, "seq", scatter_dimension=0, tiled=True)
    return attended, query_grad, total.astype(BF16)


def solution(mesh):
    in_specs = (
        P("seq", "head"),
        P("seq", None, "head"),
        P(None, None, "head"),
        P("seq", "head"),
        P(),
        P(),
    )
    out_specs = (P("seq", "head"), P("seq", "head", None), P("seq", None, "head"))
    return jax.shard_map(
        per_device, mesh=mesh, in_specs=in_specs, out_specs=out_specs, check_vma=False
    )
```

time: 322 us -> 245 us (0.76)
  matrix products: 40.4 us -> 0 us
  Pallas kernels: 0 us -> 25 us
  local copies, waits for them, and re-layouts: 38.5 us -> 14.6 us
  waiting for transfers between devices: 188 us -> 174 us
  starting transfers between devices: 21.8 us -> 8.52 us
  other arithmetic: 17.8 us -> 8.43 us
    reduce_scatter x1 -> x2, waiting for transfers between devices: 35.4 us -> 98 us  [the longest x1 53.4 us: per_device(): total = lax.psum_scatter(tiles, 'seq', scatter_dimension=0, tiled=True)]
    ppermute x2, waiting for transfers between devices: 67 us -> 7.02 us  [the longest x1 5.79 us: per_device(): edge = lax.ppermute(edge, 'seq', forward)]
    all_to_all x3 -> x1, waiting for transfers between devices: 63.6 us -> 7.84 us  [per_device(): lax.all_to_all(qgrad, 'head', split_axis=1, concat_axis=2, tiled=True)]
    dot_general x8 -> x0, matrix products: 40.4 us -> none  [the longest x1 10.1 us: per_device(): jnp.einsum('ghqk,gqhd->gkhd', probs_half, grad_pad, preferred_element_typ...]
    all_gather x1 -> x2, waiting for transfers between devices: 22 us -> 60.8 us  [the longest x1 48.1 us: per_device(): stored = lax.all_gather(encodings, 'seq', axis=0, tiled=True)]
    pallas_call x0 -> x1, Pallas kernels: none -> 25 us  [run_groups(): pl.pallas_call(group_body, grid=(groups,), in_specs=[pl.BlockSpec((parts,...]
    all_to_all x3 -> x1, starting transfers between devices: 16.3 us -> 3.47 us  [per_device(): lax.all_to_all(qgrad, 'head', split_axis=1, concat_axis=2, tiled=True)]
    another operation x3, local copies, waits for them, and re-layouts: 12.1 us -> 0.76 us  [the longest x1 0.75 us: per_device(): edge = jnp.stack([queries[-1:], grad_out[-1:]], 0)]
  transfers between devices with their start and end apart: 7 -> 7, of which waited for: 6 -> 7; matrix products, arithmetic and copies ran while one was open for 7% -> 3% of each run, Pallas kernels for 0% -> 0%
where the time goes in v1:
time: 245 us
  waiting for transfers between devices  174 us (71%)
  Pallas kernels  25 us (10%)
  local copies, waits for them, and re-layouts  14.6 us (6%)
  between operations  13.9 us (6%)
  starting transfers between devices  8.52 us (3%)
  other arithmetic  8.43 us (3%)
    reduce_scatter x1, waiting for transfers between devices, per_device(): total = lax.psum_scatter(tiles, 'seq', scatter_dimension=0, tiled=True)  53.4 us
    all_gather x1, waiting for transfers between devices, per_device(): stored = lax.all_gather(encodings, 'seq', axis=0, tiled=True)  48.1 us
    reduce_scatter x1, waiting for transfers between devices, per_device(): mine = lax.psum_scatter(term, 'head', scatter_dimension=0, tiled=True)  44.6 us
    pallas_call x1, Pallas kernels, run_groups(): pl.pallas_call(group_body, grid=(groups,), in_specs=[pl.BlockSpec((parts,...  25 us
    all_gather x1, waiting for transfers between devices, per_device(): features = lax.all_gather(picked, 'head', axis=0, tiled=False)  12.7 us
    all_to_all x1, waiting for transfers between devices, per_device(): lax.all_to_all(qgrad, 'head', split_axis=1, concat_axis=2, tiled=True)  7.84 us
    ppermute x1, waiting for transfers between devices, per_device(): edge = lax.ppermute(edge, 'seq', forward)  5.79 us
    unnamed x8, local copies, waits for them, and re-layouts  5.74 us
  transfers between devices with their start and end apart: 7, of which 7 were waited for; matrix products, arithmetic and copies ran while one was open for 3% of the time, Pallas kernels for 0%

profile of v1, /device:TPU:0, one launch (start us, length us, event | category | flops | bytes accessed | tf_op | source)
XLA Modules:
  0.0 244.9 jit_solution(7376486851268161107)
XLA Ops:
  7.2 0.7 all-gather.3.cloned.1.call-update
  7.9 0.7 multiply_add_fusion
  9.0 48.1 %all-gather.3.cloned.1.call-done = bf16[24,128,256]{2,1,0:T(8,128)(2,1)} async-done(((bf16[3,128,256]{2,1,0:T(8,128)(2,1)}), bf16[24,128,256]{2,1,0:T(8,128)(2,1)}) %all-gather.3.cloned.1.call-update) | async-done | bytes 1572880 | tf_op jit(solution)/shard_map/all_gather | solution.py:104
  57.1 2.8 %gather_fusion = bf16[8,128,256]{2,1,0:T(8,128)(2,1)} fusion(bf16[24,128,256]{2,1,0:T(8,128)(2,1)} %all-gather.3.cloned.1.call-done, s32[1024]{0:T(1024)S(1)} %pad_clamp_fusion), kind=kCustom, calls=%fused_computation | custom fusion | bytes 1048608 | tf_op jit(solution)/shard_map/gather | solution.py:105
  60.0 0.8 slice_bitcast_fusion.6
  61.3 5.8 %collective-permute-done = bf16[2,1,1024]{2,1,0:T(2,128)(2,1)S(1)} collective-permute-done((bf16[2,1,1024]{2,1,0:T(2,128)(2,1)S(1)}, bf16[2,1,1024]{2,1,0:T(2,128)(2,1)S(1)}, u32[]{:S(2)}, u32[]{:S(2)}) %collective-permute-start) | collective-permute-done | bytes 4128 | tf_op jit(solution)/shard_map/ppermute | solution.py:109
  67.1 1.6 maximum_select_fusion.1
  68.7 12.7 %all-gather.5.cloned.1.call-done.feat_ref = bf16[4,1024,256]{2,1,0:T(8,128)(2,1)} async-done(((bf16[1,1024,256]{2,1,0:T(8,128)(2,1)}), bf16[4,1024,256]{2,1,0:T(8,128)(2,1)}) %all-gather.5.cloned.1.call-update) | async-done | bytes 2097168 | tf_op jit(solution)/shard_map/all_gather | solution.py:106
  81.5 2.2 copy-done
  83.6 1.6 copy-done.2
  85.2 25.0 %shard_map.85 = (bf16[256,1024]{1,0:T(8,128)(2,1)S(1)}, bf16[256,1024]{1,0:T(8,128)(2,1)S(1)}, f32[4,1024,256]{2,1,0:T(8,128)S(1)}) custom-call(bf16[4,1024,256]{2,1,0:T(8,128)(2,1)S(1)} %copy-done.2, bf16[2,1024,1024]{2,1,0:T(8,128)(2,1)S(1)} %copy-done, bf16[256,1024]{1,0:T(8,128)(2,1)S(1)} %get-tuple-element.14.query_ref, ...), custom_call_target="tpu_custom_call" | custom-call | tf_op jit(solution)/shard_map/pallas_call | solution.py:62
  110.2 2.0 copy-done.1
  112.3 44.6 %reduce-scatter.3.cloned.1.call-done = f32[1,1024,256]{2,1,0:T(8,128)} async-done(((f32[4,1024,256]{2,1,0:T(8,128)}), f32[1,1024,256]{2,1,0:T(8,128)}) %reduce-scatter.3.cloned.1.call-update) | async-done | bytes 1048592 | tf_op jit(solution)/shard_map/reduce_scatter | solution.py:128
  156.9 2.0 broadcast_in_dim.27
  158.9 3.3 %scatter_fusion = f32[24,128,256]{2,1,0:T(8,128)} fusion(f32[24,128,256]{2,1,0:T(8,128)} %broadcast_in_dim.27, s32[8]{0:T(128)S(1)} %fusion, f32[8,128,256]{2,1,0:T(8,128)S(1)} %bitcast.32), kind=kCustom, calls=%fused_computation.1 | custom fusion | flops 262144 | bytes 3145760 | tf_op jit(solution)/shard_map/scatter-add | solution.py:130
  162.4 4.3 %collective-permute-start.1 = (bf16[2,1,1024]{2,1,0:T(2,128)(2,1)S(1)}, bf16[2,1,1024]{2,1,0:T(2,128)(2,1)S(1)}, u32[]{:S(2)}, u32[]{:S(2)}) collective-permute-start(bf16[2,1,1024]{2,1,0:T(2,128)(2,1)S(1)} %pad_maximum_fusion.3), channel_id=1, source_target_pairs={{1,0},{2,1},{3,2},{4,3},{5,4},{6,5},{7,6},{0,7},{9,8},{10,9},{11,1... | collective-permute-start | bytes 12296 | tf_op jit(solution)/shard_map/ppermute | solution.py:123
  166.8 1.2 collective-permute-done.1
  168.1 1.2 copy.14
  169.3 3.5 %all-to-all-start = ((bf16[4,64,1024]{2,0,1:T(4,128)(2,1)}), bf16[4,64,1024]{2,0,1:T(4,128)(2,1)S(1)}, u32[]{:S(2)}, u32[]{:S(2)}) async-start(bf16[4,64,1024]{2,0,1:T(4,128)(2,1)} %copy.14), calls=%async_computation | async-start | bytes 1048576 | tf_op jit(solution)/shard_map/all_to_all | solution.py:126
  172.9 0.8 pad_maximum_fusion
  173.8 7.8 %all-to-all-done = bf16[4,64,1024]{2,0,1:T(4,128)(2,1)S(1)} async-done(((bf16[4,64,1024]{2,0,1:T(4,128)(2,1)}), bf16[4,64,1024]{2,0,1:T(4,128)(2,1)S(1)}, u32[]{:S(2)}, u32[]{:S(2)}) %all-to-all-start) | async-done | bytes 524320 | tf_op jit(solution)/shard_map/all_to_all | solution.py:126
  182.0 1.2 all_to_all.16
  183.2 53.4 %reduce-scatter.5.cloned.1.call-done = f32[3,128,256]{2,1,0:T(8,128)} async-done(((f32[24,128,256]{2,1,0:T(8,128)}), f32[3,128,256]{2,1,0:T(8,128)}) %reduce-scatter.5.cloned.1.call-update) | async-done | bytes 393232 | tf_op jit(solution)/shard_map/reduce_scatter | solution.py:131
  236.6 1.7 convert_element_type.3
  (31 shorter events, 2.0 us)
Async XLA Ops:
  7.2 49.9 %all-gather.3.cloned.1.call-start = ((), (), s32[]{:S(2)}) async-start(), calls=%async_computation.3 | async-start | bytes 1769472 | tf_op jit(solution)/shard_map/all_gather | solution.py:104
  7.9 73.6 %all-gather.5.cloned.1.call-start = ((), (), s32[]{:S(2)}) async-start(), calls=%async_computation.4 | async-start | bytes 2621440 | tf_op jit(solution)/shard_map/all_gather | solution.py:106
  59.9 97.0 %reduce-scatter.3.cloned.1.call-start = ((), (), s32[]{:S(2)}) async-start(), calls=%async_computation.5 | async-start | bytes 5242880 | tf_op jit(solution)/shard_map/reduce_scatter | solution.py:128
  60.7 6.4 %collective-permute-start = (bf16[2,1,1024]{2,1,0:T(2,128)(2,1)S(1)}, bf16[2,1,1024]{2,1,0:T(2,128)(2,1)S(1)}, u32[]{:S(2)}, u32[]{:S(2)}) collective-permute-start(bf16[2,1,1024]{2,1,0:T(2,128)(2,1)S(1)} %pad_maximum_fusion.2), channel_id=1, source_target_pairs={{0,1},{1,2},{2,3},{3,4},{4,5},{5,6},{6,7},{7,0},{8,9},{9,10},{10,1... | collective-permute-start | bytes 12296 | tf_op jit(solution)/shard_map/ppermute | solution.py:109
  81.5 2.2 copy-start
  83.6 1.6 copy-start.2
  110.2 2.0 copy-start.1
  112.2 124.4 %reduce-scatter.5.cloned.1.call-start = ((), (), s32[]{:S(2)}) async-start(), calls=%async_computation.6 | async-start | bytes 3538944 | tf_op jit(solution)/shard_map/reduce_scatter | solution.py:131
  156.9 2.0 copy-start.3
  162.4 5.7 %collective-permute-start.1 = (bf16[2,1,1024]{2,1,0:T(2,128)(2,1)S(1)}, bf16[2,1,1024]{2,1,0:T(2,128)(2,1)S(1)}, u32[]{:S(2)}, u32[]{:S(2)}) collective-permute-start(bf16[2,1,1024]{2,1,0:T(2,128)(2,1)S(1)} %pad_maximum_fusion.3), channel_id=1, source_target_pairs={{1,0},{2,1},{3,2},{4,3},{5,4},{6,5},{7,6},{0,7},{9,8},{10,9},{11,1... | collective-permute-start | bytes 12296 | tf_op jit(solution)/shard_map/ppermute | solution.py:123
  169.3 12.3 %all-to-all-start = ((bf16[4,64,1024]{2,0,1:T(4,128)(2,1)}), bf16[4,64,1024]{2,0,1:T(4,128)(2,1)S(1)}, u32[]{:S(2)}, u32[]{:S(2)}) async-start(bf16[4,64,1024]{2,0,1:T(4,128)(2,1)} %copy.14), calls=%async_computation | async-start | bytes 1048576 | tf_op jit(solution)/shard_map/all_to_all | solution.py:126
Sparse Core Ops, SparseCore 0:
  10.2 46.8 all-gather.2
  60.0 21.3 all-gather.4
  112.3 44.4 reduce-scatter.2
  162.3 74.2 reduce-scatter.4

commit v2 on v1

v2 whole, which is shorter than its diff:
```python
import functools

import jax
import jax.numpy as jnp
from jax import lax
from jax.experimental import pallas as pl
from jax.experimental.pallas import tpu as pltpu
from jax.sharding import PartitionSpec as P

HEAD_DIM = 128
SPAN = 64
NEIGHBOURS = 2
NEIGHBOUR_LEN = 128
WINDOW = NEIGHBOURS * NEIGHBOUR_LEN
SCALE = HEAD_DIM ** (-0.5)
F32 = jnp.float32
BF16 = jnp.bfloat16


def dot(a, b, da, db):
    return lax.dot_general(a, b, (((da,), (db,)), ((), ())), preferred_element_type=F32)


def ring_place(index, count):
    odd = index % 2
    return (1 - odd) * (index // 2) + odd * (count - 1 - index // 2)


def ring_index(place, count):
    place = (place + 2 * count) % count
    upper = place // (count // 2)
    return (1 - upper) * 2 * place + upper * (2 * (count - 1 - place) + 1)


def meet(axis, others):
    barrier = pltpu.get_barrier_semaphore()
    for other in others:
        pl.semaphore_signal(
            barrier, inc=1, device_id={axis: other}, device_id_type=pl.DeviceIdType.MESH
        )
    pl.semaphore_wait(barrier, len(others))


def remote(src, dst, send, recv, axis, other):
    return pltpu.make_async_remote_copy(
        src_ref=src,
        dst_ref=dst,
        send_sem=send,
        recv_sem=recv,
        device_id={axis: other},
        device_id_type=pl.DeviceIdType.MESH,
    )


def gather_body(count, shard_ref, out_ref, send, recv):
    me = lax.axis_index("seq")
    place = ring_place(me, count)
    neighbours = (ring_index(place + 1, count), ring_index(place - 1, count))
    meet("seq", neighbours)
    out_ref[me] = shard_ref[...]
    rows = shard_ref.shape[1] // 2
    hops = ((count // 2, count // 2 - 1), (count // 2 - 1, count // 2))

    def copy(way, half, step):
        owner = ring_index(place - step if way == 0 else place + step, count)
        ref = out_ref.at[owner, :, pl.ds(half * rows, rows), :]
        return remote(
            ref, ref, send.at[way, half, step], recv.at[way, half, step], "seq", neighbours[way]
        )

    lanes = [(way, half) for half in range(2) for way in range(2)]
    for step in range(count // 2):
        for way, half in lanes:
            if step < hops[way][half]:
                if step > 0:
                    copy(way, half, step - 1).wait_recv()
                copy(way, half, step).start()
    for way, half in lanes:
        copy(way, half, hops[way][half] - 1).wait_recv()
        for step in range(hops[way][half]):
            copy(way, half, step).wait_send()


def gather_tiles(shard, count):
    tiles, rows, part = shard.shape
    return pl.pallas_call(
        functools.partial(gather_body, count),
        in_specs=[pl.BlockSpec(memory_space=pltpu.VMEM)],
        out_specs=pl.BlockSpec(memory_space=pltpu.VMEM),
        out_shape=jax.ShapeDtypeStruct((count, tiles, rows, part), shard.dtype),
        scratch_shapes=[
            pltpu.SemaphoreType.DMA((2, 2, count // 2)),
            pltpu.SemaphoreType.DMA((2, 2, count // 2)),
        ],
        compiler_params=pltpu.CompilerParams(
            collective_id=0, has_side_effects=True, vmem_limit_bytes=32 << 20
        ),
    )(shard)


def scatter_body(count, share_ref, mine_ref, out_ref, buf, send, recv):
    me = lax.axis_index("seq")
    place = ring_place(me, count)
    neighbours = (ring_index(place + 1, count), ring_index(place - 1, count))
    meet("seq", neighbours)
    tiles, length, _ = out_ref.shape
    requests = mine_ref.shape[0]
    rows = length // 2

    def own(way, target, k):
        total = None
        for r in range(requests):
            piece = share_ref[target * tiles + k, r] * mine_ref[r, way * rows : (way + 1) * rows, :]
            total = piece if total is None else total + piece
        return total

    def target_of(way, step):
        return ring_index(place - 1 - step if way == 0 else place + 1 + step, count)

    def copy(way, step, k):
        return remote(
            buf.at[way, step, k],
            buf.at[way, step + 1, k],
            send.at[way, step, k],
            recv.at[way, step, k],
            "seq",
            neighbours[way],
        )

    for k in range(tiles):
        for way in range(2):
            buf[way, 0, k] = own(way, target_of(way, 0), k)
            copy(way, 0, k).start()

    def step_body(step, carry):
        for k in range(tiles):
            for way in range(2):
                piece = own(way, target_of(way, step), k)
                copy(way, step - 1, k).wait_recv()
                buf[way, step, k] = buf[way, step, k] + piece
                copy(way, step, k).start()
        return carry

    lax.fori_loop(1, count - 1, step_body, 0)
    for k in range(tiles):
        for way in range(2):
            piece = own(way, me, k)
            copy(way, count - 2, k).wait_recv()
            out_ref[k, way * rows : (way + 1) * rows, :] = (buf[way, count - 1, k] + piece).astype(
                out_ref.dtype
            )

    def drain(step, carry):
        for k in range(tiles):
            for way in range(2):
                copy(way, step, k).wait_send()
        return carry

    lax.fori_loop(0, count - 1, drain, 0)


def scatter_tiles(share, mine, count, tiles):
    _, length, part = mine.shape
    return pl.pallas_call(
        functools.partial(scatter_body, count),
        in_specs=[
            pl.BlockSpec(memory_space=pltpu.SMEM),
            pl.BlockSpec(memory_space=pltpu.VMEM),
        ],
        out_specs=pl.BlockSpec(memory_space=pltpu.VMEM),
        out_shape=jax.ShapeDtypeStruct((tiles, length, part), BF16),
        scratch_shapes=[
            pltpu.VMEM((2, count, tiles, length // 2, part), F32),
            pltpu.SemaphoreType.DMA((2, count - 1, tiles)),
            pltpu.SemaphoreType.DMA((2, count - 1, tiles)),
        ],
        compiler_params=pltpu.CompilerParams(
            collective_id=2, has_side_effects=True, vmem_limit_bytes=32 << 20
        ),
    )(share, mine)


def group_body(
    parts, feat_ref, weight_ref, query_ref, grad_ref, att_ref, qgrad_ref, out_ref,
    kv, kv_grad, term, from_core, across, from_chip, core_send, core_recv, chip_send, chip_recv,
):
    head = lax.axis_index("head")
    core, chip = head % 2, head // 2
    chips = parts // 2
    sibling = chip * 2 + 1 - core
    peers = [((chip + d) % chips) * 2 + core for d in range(1, chips)]
    meet("head", [sibling] + peers)
    part = feat_ref.shape[2]
    width = query_ref.shape[1]
    groups = query_ref.shape[0] // SPAN

    def to_core(i):
        return remote(
            term.at[i, 1 - core], from_core.at[i], core_send.at[i], core_recv.at[i], "head", sibling
        )

    def to_chip(i, d):
        return remote(
            across.at[i, d - 1],
            from_chip.at[i, d - 1],
            chip_send.at[i, d - 1],
            chip_recv.at[i, d - 1],
            "head",
            peers[d - 1],
        )

    def pass_on(i):
        to_core(i).wait_recv()
        for d in range(1, chips):
            target = (chip + d) % chips
            across[i, d - 1] = term[i, core, target] + from_core[i, target]
            to_chip(i, d).start()

    def group(i, carry):
        keys = pl.ds(pl.multiple_of(i * WINDOW, WINDOW), WINDOW)
        tokens = pl.ds(pl.multiple_of(i * SPAN, SPAN), SPAN)
        for c in range(2):
            total = None
            for j in range(parts):
                piece = dot(feat_ref[j, keys, :], weight_ref[c, j * part : (j + 1) * part, :], 1, 0)
                total = piece if total is None else total + piece
            kv[c] = total.astype(BF16)
        for h in range(width // HEAD_DIM):
            cols = slice(h * HEAD_DIM, (h + 1) * HEAD_DIM)
            q = query_ref[tokens, cols]
            g = grad_ref[tokens, cols]
            k = kv[0, :, cols]
            v = kv[1, :, cols]
            scores = dot(q, k, 1, 1) * SCALE
            dprob = dot(g, v, 1, 1)
            expo = jnp.exp(scores - jnp.max(scores, axis=-1, keepdims=True))
            probs = expo / jnp.sum(expo, axis=-1, keepdims=True)
            half = probs.astype(BF16)
            delta = jnp.sum(probs * dprob, axis=-1, keepdims=True)
            dscore = (probs * (dprob - delta)).astype(BF16)
            att_ref[tokens, cols] = dot(half, v, 1, 0).astype(BF16)
            qgrad_ref[tokens, cols] = (dot(dscore, k, 1, 0) * SCALE).astype(BF16)
            kv_grad[0, :, cols] = (dot(dscore, q, 0, 0) * SCALE).astype(BF16)
            kv_grad[1, :, cols] = dot(half, g, 0, 0).astype(BF16)
        for j in range(parts):
            rows = slice(j * part, (j + 1) * part)
            term[i, j % 2, j // 2] = dot(kv_grad[0], weight_ref[0, rows, :], 1, 1) + dot(
                kv_grad[1], weight_ref[1, rows, :], 1, 1
            )
        to_core(i).start()

        @pl.when(i > 0)
        def _():
            pass_on(i - 1)

        return carry

    lax.fori_loop(0, groups, group, 0)
    pass_on(groups - 1)
    for i in range(groups):
        total = term[i, core, chip] + from_core[i, chip]
        for d in range(1, chips):
            to_chip(i, d).wait_recv()
            total = total + from_chip[i, d - 1]
        out_ref[i * WINDOW : (i + 1) * WINDOW, :] = total
    for i in range(groups):
        to_core(i).wait_send()
        for d in range(1, chips):
            to_chip(i, d).wait_send()


def run_groups(features, kv_weight, query_rows, grad_rows):
    parts, rows, part = features.shape
    token_rows, width = query_rows.shape
    groups = token_rows // SPAN
    chips = parts // 2
    vmem = pl.BlockSpec(memory_space=pltpu.VMEM)
    return pl.pallas_call(
        functools.partial(group_body, parts),
        in_specs=[vmem] * 4,
        out_specs=[vmem] * 3,
        out_shape=[
            jax.ShapeDtypeStruct((token_rows, width), BF16),
            jax.ShapeDtypeStruct((token_rows, width), BF16),
            jax.ShapeDtypeStruct((rows, part), F32),
        ],
        scratch_shapes=[
            pltpu.VMEM((2, WINDOW, width), BF16),
            pltpu.VMEM((2, WINDOW, width), BF16),
            pltpu.VMEM((groups, 2, chips, WINDOW, part), F32),
            pltpu.VMEM((groups, chips, WINDOW, part), F32),
            pltpu.VMEM((groups, chips - 1, WINDOW, part), F32),
            pltpu.VMEM((groups, chips - 1, WINDOW, part), F32),
            pltpu.SemaphoreType.DMA((groups,)),
            pltpu.SemaphoreType.DMA((groups,)),
            pltpu.SemaphoreType.DMA((groups, chips - 1)),
            pltpu.SemaphoreType.DMA((groups, chips - 1)),
        ],
        compiler_params=pltpu.CompilerParams(
            collective_id=1, has_side_effects=True, vmem_limit_bytes=48 << 20
        ),
    )(features, kv_weight, query_rows, grad_rows)


def per_device(queries, encodings, kv_weight, grad_out, neighbour_owner, neighbour_slot):
    seq_count = lax.axis_size("seq")
    seq_index = lax.axis_index("seq")
    token_rows, width = queries.shape
    requests = token_rows // SPAN * NEIGHBOURS
    tile_rows, _, part = encodings.shape
    forward = [(i, (i + 1) % seq_count) for i in range(seq_count)]
    backward = [((i + 1) % seq_count, i) for i in range(seq_count)]

    tile = neighbour_owner * tile_rows + neighbour_slot
    tile = jnp.roll(tile, 1, axis=0).reshape(seq_count, requests)
    tile = lax.dynamic_index_in_dim(tile, seq_index, 0, keepdims=False)

    stored = gather_tiles(encodings, seq_count).reshape(-1, NEIGHBOUR_LEN, part)
    picked = stored[tile].reshape(requests * NEIGHBOUR_LEN, part)
    features = lax.all_gather(picked, "head", axis=0, tiled=False)

    edge = jnp.stack([queries[-1:], grad_out[-1:]], 0)
    edge = lax.ppermute(edge, "seq", forward)
    row = lax.broadcasted_iota(jnp.int32, (token_rows, 1), 0)
    unattending = (seq_index == 0) & (row >= 1) & (row < SPAN)
    zero = jnp.zeros((), BF16)

    def shifted(rows, first):
        rows = jnp.concatenate([first, rows[:-1]], 0)
        return jnp.where(unattending, zero, rows)

    query_rows = shifted(queries, edge[0])
    grad_rows = shifted(grad_out, edge[1])
    att, qgrad, mine = run_groups(features, kv_weight, query_rows, grad_rows)

    att = jnp.where(unattending, zero, att)
    last = lax.ppermute(jnp.stack([att[:1], qgrad[:1]], 0), "seq", backward)
    attended = jnp.concatenate([att[1:], last[0]], 0)
    qgrad = jnp.concatenate([qgrad[1:], last[1]], 0).reshape(-1, SPAN, width)
    query_grad = lax.all_to_all(qgrad, "head", split_axis=1, concat_axis=2, tiled=True)

    mine = mine.reshape(requests, NEIGHBOUR_LEN, part)
    share = (jnp.arange(seq_count * tile_rows)[:, None] == tile[None, :]).astype(F32)
    total = scatter_tiles(share, mine, seq_count, tile_rows)
    return attended, query_grad, total


def solution(mesh):
    in_specs = (
        P("seq", "head"),
        P("seq", None, "head"),
        P(None, None, "head"),
        P("seq", "head"),
        P(),
        P(),
    )
    out_specs = (P("seq", "head"), P("seq", "head", None), P("seq", None, "head"))
    return jax.shard_map(
        per_device, mesh=mesh, in_specs=in_specs, out_specs=out_specs, check_vma=False
    )
```

time: 245 us -> 156 us (0.64)
  waiting for transfers between devices: 174 us -> 22.3 us
  Pallas kernels: 25 us -> 100 us
  local copies, waits for them, and re-layouts: 14.6 us -> 7.9 us
  other arithmetic: 8.43 us -> 2.22 us
    reduce_scatter x2 -> x0, waiting for transfers between devices: 98 us -> none  [the longest x1 53.4 us: per_device(): total = lax.psum_scatter(tiles, 'seq', scatter_dimension=0, tiled=True)]
    pallas_call x1 -> x3, Pallas kernels: 25 us -> 100 us  [the longest x1 41.1 us: run_groups(): pl.pallas_call(functools.partial(group_body, parts), in_specs=[vmem] * 4,...]
    all_gather x1 -> x0, waiting for transfers between devices: 48.1 us -> none  [per_device(): stored = lax.all_gather(encodings, 'seq', axis=0, tiled=True)]
    all_to_all x1, waiting for transfers between devices: 7.84 us -> 0.01 us  [per_device(): lax.all_to_all(qgrad, 'head', split_axis=1, concat_axis=2, tiled=True)]
    scatter-add x1 -> x0, other arithmetic: 3.3 us -> none  [per_device(): jnp.zeros((seq_count * tile_rows, NEIGHBOUR_LEN, part), F32).at[tile]]
    all_gather x1, waiting for transfers between devices: 12.7 us -> 15.7 us  [per_device(): features = lax.all_gather(picked, 'head', axis=0, tiled=False)]
    unnamed x8 -> x9, local copies, waits for them, and re-layouts: 5.74 us -> 3.2 us
  transfers between devices with their start and end apart: 7 -> 4, of which waited for: 7 -> 3; matrix products, arithmetic and copies ran while one was open for 3% -> 1% of each run, Pallas kernels for 0% -> 23%
where the time goes in v2:
time: 156 us
  Pallas kernels  100 us (64%)
  waiting for transfers between devices  22.3 us (14%)
  between operations  14.2 us (9%)
  starting transfers between devices  8.83 us (6%)
  local copies, waits for them, and re-layouts  7.9 us (5%)
  other arithmetic  2.22 us (1%)
    pallas_call x1, Pallas kernels, run_groups(): pl.pallas_call(functools.partial(group_body, parts), in_specs=[vmem] * 4,...  41.1 us
    pallas_call x1, Pallas kernels, scatter_tiles(): pl.pallas_call(functools.partial(scatter_body, count), in_specs=[pl.Block...  36 us
    pallas_call x1, Pallas kernels, gather_tiles(): pl.pallas_call(functools.partial(gather_body, count), in_specs=[pl.BlockS...  23.2 us
    all_gather x1, waiting for transfers between devices, per_device(): features = lax.all_gather(picked, 'head', axis=0, tiled=False)  15.7 us
    ppermute x1, waiting for transfers between devices, per_device(): edge = lax.ppermute(edge, 'seq', forward)  5.36 us
    ppermute x1, starting transfers between devices, per_device(): last = lax.ppermute(jnp.stack([att[:1], qgrad[:1]], 0), 'seq', backward)  4.29 us
    all_to_all x1, starting transfers between devices, per_device(): lax.all_to_all(qgrad, 'head', split_axis=1, concat_axis=2, tiled=True)  3.47 us
    unnamed x9, local copies, waits for them, and re-layouts  3.2 us
  transfers between devices with their start and end apart: 4, of which 3 were waited for; matrix products, arithmetic and copies ran while one was open for 1% of the time, Pallas kernels for 23%

profile of v2, /device:TPU:0, one launch (start us, length us, event | category | flops | bytes accessed | tf_op | source)
XLA Modules:
  0.0 155.8 jit_solution(12026458358530517448)
XLA Ops:
  7.2 0.7 multiply_add_fusion
  8.0 0.1 pad_add_fusion
  8.1 0.1 copy.13
  8.3 0.9 copy-done.1
  9.2 23.2 %shard_map.85 = bf16[8,3,128,256]{3,2,1,0:T(8,128)(2,1)S(1)} custom-call(bf16[3,128,256]{2,1,0:T(8,128)(2,1)S(1)} %copy-done.1), custom_call_target="tpu_custom_call" | custom-call | tf_op jit(solution)/shard_map/pallas_call | solution.py:86
  32.4 1.4 gather_fusion
  33.8 1.0 collective-permute-start
  34.9 5.4 %collective-permute-done = bf16[2,1,1024]{2,1,0:T(2,128)(2,1)S(1)} collective-permute-done((bf16[2,1,1024]{2,1,0:T(2,128)(2,1)S(1)}, bf16[2,1,1024]{2,1,0:T(2,128)(2,1)S(1)}, u32[]{:S(2)}, u32[]{:S(2)}) %collective-permute-start) | collective-permute-done | bytes 4128 | tf_op jit(solution)/shard_map/ppermute | solution.py:323
  40.2 0.4 maximum_select_fusion.1
  40.6 15.7 %all-gather.2.cloned.1.call-done.feat_ref = bf16[4,1024,256]{2,1,0:T(8,128)(2,1)} async-done(((bf16[1,1024,256]{2,1,0:T(8,128)(2,1)}), bf16[4,1024,256]{2,1,0:T(8,128)(2,1)}) %all-gather.2.cloned.1.call-update) | async-done | bytes 2097168 | tf_op jit(solution)/shard_map/all_gather | solution.py:320
  56.4 1.6 %copy-done = bf16[4,1024,256]{2,1,0:T(8,128)(2,1)S(1)} copy-done((bf16[4,1024,256]{2,1,0:T(8,128)(2,1)S(1)}, bf16[4,1024,256]{2,1,0:T(8,128)(2,1)}, u32[]{:S(2)}) %copy-start) | copy-done | bytes 2097176
  58.0 41.1 %shard_map.86 = (bf16[256,1024]{1,0:T(8,128)(2,1)S(1)}, bf16[256,1024]{1,0:T(8,128)(2,1)S(1)}, f32[1024,256]{1,0:T(8,128)S(1)}) custom-call(bf16[4,1024,256]{2,1,0:T(8,128)(2,1)S(1)} %copy-done, bf16[2,1024,1024]{2,1,0:T(8,128)(2,1)} %weight_ref.1, bf16[256,1024]{1,0:T(8,128)(2,1)S(1)} %get-tuple-element.14.query_ref, ...), custom_call_target="tpu_custom_call" | custom-call | tf_op jit(solution)/shard_map/pallas_call | solution.py:278
  99.1 0.1 broadcast_select_fusion
  99.2 4.3 %collective-permute-start.1 = (bf16[2,1,1024]{2,1,0:T(2,128)(2,1)S(1)}, bf16[2,1,1024]{2,1,0:T(2,128)(2,1)S(1)}, u32[]{:S(2)}, u32[]{:S(2)}) collective-permute-start(bf16[2,1,1024]{2,1,0:T(2,128)(2,1)S(1)} %pad_maximum_fusion.3), channel_id=1, source_target_pairs={{1,0},{2,1},{3,2},{4,3},{5,4},{6,5},{7,6},{0,7},{9,8},{10,9},{11,1... | collective-permute-start | bytes 12296 | tf_op jit(solution)/shard_map/ppermute | solution.py:337
  103.5 0.1 slice.56
  103.7 1.2 collective-permute-done.1
  105.0 1.2 copy.14
  106.2 3.5 %all-to-all-start = ((bf16[4,64,1024]{2,0,1:T(4,128)(2,1)}), bf16[4,64,1024]{2,0,1:T(4,128)(2,1)S(1)}, u32[]{:S(2)}, u32[]{:S(2)}) async-start(bf16[4,64,1024]{2,0,1:T(4,128)(2,1)} %copy.14), calls=%async_computation | async-start | bytes 1048576 | tf_op jit(solution)/shard_map/all_to_all | solution.py:340
  109.7 0.1 slice.62
  109.8 36.0 %shard_map.87 = bf16[3,128,256]{2,1,0:T(8,128)(2,1)S(1)} custom-call(f32[24,8]{1,0:T(8,128)S(1)} %fusion.share_ref, f32[8,128,256]{2,1,0:T(8,128)S(1)} %bitcast.33), custom_call_target="tpu_custom_call" | custom-call | tf_op jit(solution)/shard_map/pallas_call | solution.py:164
  145.9 0.8 pad_maximum_fusion
  146.7 0.4 copy.15
  147.1 1.2 all_to_all.16
  148.3 0.7 copy.17
  (24 shorter events, 0.4 us)
Async XLA Ops:
  7.2 49.2 %all-gather.2.cloned.1.call-start = ((), (), s32[]{:S(2)}) async-start(), calls=%async_computation.1 | async-start | bytes 2621440 | tf_op jit(solution)/shard_map/all_gather | solution.py:320
  8.3 0.9 copy-start.1
  9.2 24.6 %copy-start.2 = (bf16[256,1024]{1,0:T(8,128)(2,1)S(1)}, bf16[256,1024]{1,0:T(8,128)(2,1)}, u32[]{:S(2)}) copy-start(bf16[256,1024]{1,0:T(8,128)(2,1)} %param.9) | copy-start | bytes 1572868
  9.2 24.6 %copy-start.3 = (bf16[256,1024]{1,0:T(8,128)(2,1)S(1)}, bf16[256,1024]{1,0:T(8,128)(2,1)}, u32[]{:S(2)}) copy-start(bf16[256,1024]{1,0:T(8,128)(2,1)} %param.6) | copy-start | bytes 1572868
  33.8 6.4 %collective-permute-start = (bf16[2,1,1024]{2,1,0:T(2,128)(2,1)S(1)}, bf16[2,1,1024]{2,1,0:T(2,128)(2,1)S(1)}, u32[]{:S(2)}, u32[]{:S(2)}) collective-permute-start(bf16[2,1,1024]{2,1,0:T(2,128)(2,1)S(1)} %pad_maximum_fusion.2), channel_id=1, source_target_pairs={{0,1},{1,2},{2,3},{3,4},{4,5},{5,6},{6,7},{7,0},{8,9},{9,10},{10,1... | collective-permute-start | bytes 12296 | tf_op jit(solution)/shard_map/ppermute | solution.py:323
  56.4 1.6 %copy-start = (bf16[4,1024,256]{2,1,0:T(8,128)(2,1)S(1)}, bf16[4,1024,256]{2,1,0:T(8,128)(2,1)}, u32[]{:S(2)}) copy-start(bf16[4,1024,256]{2,1,0:T(8,128)(2,1)} %all-gather.2.cloned.1.call-done.feat_ref) | copy-start | bytes 6291460
  99.2 5.7 %collective-permute-start.1 = (bf16[2,1,1024]{2,1,0:T(2,128)(2,1)S(1)}, bf16[2,1,1024]{2,1,0:T(2,128)(2,1)S(1)}, u32[]{:S(2)}, u32[]{:S(2)}) collective-permute-start(bf16[2,1,1024]{2,1,0:T(2,128)(2,1)S(1)} %pad_maximum_fusion.3), channel_id=1, source_target_pairs={{1,0},{2,1},{3,2},{4,3},{5,4},{6,5},{7,6},{0,7},{9,8},{10,9},{11,1... | collective-permute-start | bytes 12296 | tf_op jit(solution)/shard_map/ppermute | solution.py:337
  106.2 40.5 %all-to-all-start = ((bf16[4,64,1024]{2,0,1:T(4,128)(2,1)}), bf16[4,64,1024]{2,0,1:T(4,128)(2,1)S(1)}, u32[]{:S(2)}, u32[]{:S(2)}) async-start(bf16[4,64,1024]{2,0,1:T(4,128)(2,1)} %copy.14), calls=%async_computation | async-start | bytes 1048576 | tf_op jit(solution)/shard_map/all_to_all | solution.py:340
Sparse Core Ops, SparseCore 0:
  33.9 22.4 all-gather.1

commit v3 on v2

--- a/solution.py
+++ b/solution.py
@@ -32,9 +32,9 @@
     return (1 - upper) * 2 * place + upper * (2 * (count - 1 - place) + 1)
 
 
-def meet(axis, others):
+def meet(others):
     barrier = pltpu.get_barrier_semaphore()
-    for other in others:
+    for axis, other in others:
         pl.semaphore_signal(
             barrier, inc=1, device_id={axis: other}, device_id_type=pl.DeviceIdType.MESH
         )
@@ -52,57 +52,75 @@
     )
 
 
-def gather_body(count, shard_ref, out_ref, send, recv):
+def gather_body(
+    count, pick_ref, shard_ref, edge_ref, picked_ref, edge_out, stored, send, recv, edge_send, edge_recv
+):
     me = lax.axis_index("seq")
     place = ring_place(me, count)
     neighbours = (ring_index(place + 1, count), ring_index(place - 1, count))
-    meet("seq", neighbours)
-    out_ref[me] = shard_ref[...]
+    after = (me + 1) % count
+    before = (me + count - 1) % count
+    meet([("seq", other) for other in neighbours + (after, before)])
+    stored[me] = shard_ref[...]
     rows = shard_ref.shape[1] // 2
     hops = ((count // 2, count // 2 - 1), (count // 2 - 1, count // 2))
 
     def copy(way, half, step):
         owner = ring_index(place - step if way == 0 else place + step, count)
-        ref = out_ref.at[owner, :, pl.ds(half * rows, rows), :]
+        ref = stored.at[owner, :, pl.ds(half * rows, rows), :]
         return remote(
             ref, ref, send.at[way, half, step], recv.at[way, half, step], "seq", neighbours[way]
         )
 
     lanes = [(way, half) for half in range(2) for way in range(2)]
+    edge = remote(edge_ref, edge_out, edge_send.at[0], edge_recv.at[0], "seq", after)
     for step in range(count // 2):
         for way, half in lanes:
             if step < hops[way][half]:
                 if step > 0:
                     copy(way, half, step - 1).wait_recv()
                 copy(way, half, step).start()
+        if step == 0:
+            edge.start()
     for way, half in lanes:
         copy(way, half, hops[way][half] - 1).wait_recv()
+    for r in range(picked_ref.shape[0]):
+        picked_ref[r] = stored[pick_ref[0, r], pick_ref[1, r]]
+    edge.wait()
+    for way, half in lanes:
         for step in range(hops[way][half]):
             copy(way, half, step).wait_send()
 
 
-def gather_tiles(shard, count):
+def gather_tiles(pick, shard, edge, count):
     tiles, rows, part = shard.shape
+    vmem = pl.BlockSpec(memory_space=pltpu.VMEM)
     return pl.pallas_call(
         functools.partial(gather_body, count),
-        in_specs=[pl.BlockSpec(memory_space=pltpu.VMEM)],
-        out_specs=pl.BlockSpec(memory_space=pltpu.VMEM),
-        out_shape=jax.ShapeDtypeStruct((count, tiles, rows, part), shard.dtype),
+        in_specs=[pl.BlockSpec(memory_space=pltpu.SMEM), vmem, vmem],
+        out_specs=[vmem, vmem],
+        out_shape=[
+            jax.ShapeDtypeStruct((pick.shape[1], rows, part), shard.dtype),
+            jax.ShapeDtypeStruct(edge.shape, edge.dtype),
+        ],
         scratch_shapes=[
+            pltpu.VMEM((count, tiles, rows, part), shard.dtype),
             pltpu.SemaphoreType.DMA((2, 2, count // 2)),
             pltpu.SemaphoreType.DMA((2, 2, count // 2)),
+            pltpu.SemaphoreType.DMA((1,)),
+            pltpu.SemaphoreType.DMA((1,)),
         ],
         compiler_params=pltpu.CompilerParams(
             collective_id=0, has_side_effects=True, vmem_limit_bytes=32 << 20
         ),
-    )(shard)
+    )(pick, shard, edge)
 
 
 def scatter_body(count, share_ref, mine_ref, out_ref, buf, send, recv):
     me = lax.axis_index("seq")
     place = ring_place(me, count)
     neighbours = (ring_index(place + 1, count), ring_index(place - 1, count))
-    meet("seq", neighbours)
+    meet([("seq", other) for other in neighbours])
     tiles, length, _ = out_ref.shape
     requests = mine_ref.shape[0]
     rows = length // 2
@@ -181,18 +199,53 @@
 
 
 def group_body(
-    parts, feat_ref, weight_ref, query_ref, grad_ref, att_ref, qgrad_ref, out_ref,
-    kv, kv_grad, term, from_core, across, from_chip, core_send, core_recv, chip_send, chip_recv,
+    parts, count, picked_ref, weight_ref, query_ref, grad_ref, edge_ref,
+    att_ref, qgrad_ref, out_ref,
+    feat, kv, kv_grad, rows_in, tail, att_rows, qgrad_rows, edge_out, edge_in, qout, qin,
+    term, from_core, across, from_chip,
+    pick_send, pick_recv, far_send, far_recv, pass_send, pass_recv,
+    edge_send, edge_recv, q_send, q_recv, core_send, core_recv, chip_send, chip_recv,
 ):
     head = lax.axis_index("head")
+    seq = lax.axis_index("seq")
     core, chip = head % 2, head // 2
     chips = parts // 2
     sibling = chip * 2 + 1 - core
     peers = [((chip + d) % chips) * 2 + core for d in range(1, chips)]
-    meet("head", [sibling] + peers)
-    part = feat_ref.shape[2]
+    others = [(head + d) % parts for d in range(1, parts)]
+    before = (seq + count - 1) % count
+    after = (seq + 1) % count
+    meet([("head", other) for other in others] + [("seq", before), ("seq", after)])
+    part = picked_ref.shape[2]
     width = query_ref.shape[1]
     groups = query_ref.shape[0] // SPAN
+    segment = SPAN // parts
+
+    def to_sibling(i):
+        return remote(
+            picked_ref.at[i], feat.at[head, i], pick_send.at[i], pick_recv.at[i], "head", sibling
+        )
+
+    def to_far(i, d):
+        return remote(
+            picked_ref.at[i],
+            feat.at[head, i],
+            far_send.at[i, d - 1],
+            far_recv.at[i, d - 1],
+            "head",
+            peers[d - 1],
+        )
+
+    def pass_far(i, d):
+        ref = feat.at[((chip + chips - d) % chips) * 2 + core, i]
+        return remote(
+            ref, ref, pass_send.at[i, d - 1], pass_recv.at[i, d - 1], "head", sibling
+        )
+
+    def hand_over(i):
+        for d in range(1, chips):
+            to_far(i, d).wait_recv()
+            pass_far(i, d).start()
 
     def to_core(i):
         return remote(
@@ -209,6 +262,18 @@
             peers[d - 1],
         )
 
+    def to_head(i, d):
+        return remote(
+            qout.at[i, others[d - 1]],
+            qin.at[head, i],
+            q_send.at[i, d - 1],
+            q_recv.at[i, d - 1],
+            "head",
+            others[d - 1],
+        )
+
+    edge = remote(edge_out, edge_in, edge_send.at[0], edge_recv.at[0], "seq", before)
+
     def pass_on(i):
         to_core(i).wait_recv()
         for d in range(1, chips):
@@ -216,19 +281,56 @@
             across[i, d - 1] = term[i, core, target] + from_core[i, target]
             to_chip(i, d).start()
 
+    last16 = lax.broadcasted_iota(jnp.int32, (16, width), 0) == 15
+    last_segment = lax.broadcasted_iota(jnp.int32, (segment, width), 0) == segment - 1
+    place = lax.broadcasted_iota(jnp.int32, (SPAN, width), 0)
+
+    def finish_span(i, att16, qgrad16):
+        rows = pl.ds(pl.multiple_of(i * SPAN + SPAN - 16, 16), 16)
+        att_ref[rows, :] = jnp.where(last16, att16, att_ref[rows, :].astype(F32)).astype(BF16)
+        qout[i, parts - 1] = jnp.where(
+            last_segment, qgrad16[16 - segment :], qout[i, parts - 1].astype(F32)
+        ).astype(BF16)
+        qin[head, i] = qout[i, head]
+        for d in range(1, parts):
+            to_head(i, d).start()
+
+    for i in range(groups):
+        for d in range(1, chips):
+            to_far(i, d).start()
+        to_sibling(i).start()
+    for i in range(groups):
+        feat[head, i] = picked_ref[i]
+    tail[...] = edge_ref[...]
+    hand_over(0)
+
     def group(i, carry):
-        keys = pl.ds(pl.multiple_of(i * WINDOW, WINDOW), WINDOW)
         tokens = pl.ds(pl.multiple_of(i * SPAN, SPAN), SPAN)
+        limit = jnp.where(jnp.logical_and(seq == 0, i == 0), SPAN - 1, 0)
+        for c, ref in ((0, query_ref), (1, grad_ref)):
+            rows = ref[tokens, :].astype(F32)
+            ending = jnp.where(last16, tail[c].astype(F32), rows[SPAN - 16 :])
+            tail[c] = rows[SPAN - 16 :].astype(BF16)
+            rows = jnp.concatenate([rows[: SPAN - 16], ending], 0)
+            rows_in[c] = jnp.where(place >= limit, rows, 0.0).astype(BF16)
+        to_sibling(i).wait_recv()
+        for d in range(1, chips):
+            pass_far(i, d).wait_recv()
         for c in range(2):
             total = None
             for j in range(parts):
-                piece = dot(feat_ref[j, keys, :], weight_ref[c, j * part : (j + 1) * part, :], 1, 0)
+                piece = dot(feat[j, i], weight_ref[c, j * part : (j + 1) * part, :], 1, 0)
                 total = piece if total is None else total + piece
             kv[c] = total.astype(BF16)
+
+        @pl.when(i + 1 < groups)
+        def _():
+            hand_over(i + 1)
+
         for h in range(width // HEAD_DIM):
             cols = slice(h * HEAD_DIM, (h + 1) * HEAD_DIM)
-            q = query_ref[tokens, cols]
-            g = grad_ref[tokens, cols]
+            q = rows_in[0, :, cols]
+            g = rows_in[1, :, cols]
             k = kv[0, :, cols]
             v = kv[1, :, cols]
             scores = dot(q, k, 1, 1) * SCALE
@@ -238,8 +340,8 @@
             half = probs.astype(BF16)
             delta = jnp.sum(probs * dprob, axis=-1, keepdims=True)
             dscore = (probs * (dprob - delta)).astype(BF16)
-            att_ref[tokens, cols] = dot(half, v, 1, 0).astype(BF16)
-            qgrad_ref[tokens, cols] = (dot(dscore, k, 1, 0) * SCALE).astype(BF16)
+            att_rows[:, cols] = dot(half, v, 1, 0)
+            qgrad_rows[:, cols] = dot(dscore, k, 1, 0) * SCALE
             kv_grad[0, :, cols] = (dot(dscore, q, 0, 0) * SCALE).astype(BF16)
             kv_grad[1, :, cols] = dot(half, g, 0, 0).astype(BF16)
         for j in range(parts):
@@ -248,98 +350,123 @@
                 kv_grad[1], weight_ref[1, rows, :], 1, 1
             )
         to_core(i).start()
+        att = jnp.where(place >= limit, att_rows[...], 0.0)
+        att_ref[tokens, :] = att.astype(BF16)
+        for j in range(parts):
+            qout[i, j] = qgrad_rows[j * segment : (j + 1) * segment, :].astype(BF16)
+
+        @pl.when(i == 0)
+        def _():
+            edge_out[0] = att_rows[SPAN - 16 :, :].astype(BF16)
+            edge_out[1] = qgrad_rows[SPAN - 16 :, :].astype(BF16)
+            edge.start()
 
         @pl.when(i > 0)
         def _():
             pass_on(i - 1)
+            finish_span(i - 1, att_rows[SPAN - 16 :, :], qgrad_rows[SPAN - 16 :, :])
 
         return carry
 
     lax.fori_loop(0, groups, group, 0)
     pass_on(groups - 1)
+    edge.wait_recv()
+    finish_span(groups - 1, edge_in[0].astype(F32), edge_in[1].astype(F32))
     for i in range(groups):
         total = term[i, core, chip] + from_core[i, chip]
         for d in range(1, chips):
             to_chip(i, d).wait_recv()
             total = total + from_chip[i, d - 1]
         out_ref[i * WINDOW : (i + 1) * WINDOW, :] = total
+    edge.wait_send()
+    for i in range(groups):
+        for d in range(1, parts):
+            to_head(i, d).wait_recv()
+        for j in range(parts):
+            qgrad_ref[i, :, j * width : (j + 1) * width] = qin[j, i]
     for i in range(groups):
         to_core(i).wait_send()
+        to_sibling(i).wait_send()
         for d in range(1, chips):
             to_chip(i, d).wait_send()
-
-
-def run_groups(features, kv_weight, query_rows, grad_rows):
-    parts, rows, part = features.shape
-    token_rows, width = query_rows.shape
-    groups = token_rows // SPAN
+            to_far(i, d).wait_send()
+            pass_far(i, d).wait_send()
+        for d in range(1, parts):
+            to_head(i, d).wait_send()
+
+
+def run_groups(picked, kv_weight, queries, grad_out, edge, parts, count):
+    groups, rows, part = picked.shape
+    token_rows, width = queries.shape
     chips = parts // 2
+    segment = SPAN // parts
     vmem = pl.BlockSpec(memory_space=pltpu.VMEM)
+    dma = pltpu.SemaphoreType.DMA
     return pl.pallas_call(
-        functools.partial(group_body, parts),
-        in_specs=[vmem] * 4,
+        functools.partial(group_body, parts, count),
+        in_specs=[vmem] * 5,
         out_specs=[vmem] * 3,
         out_shape=[
             jax.ShapeDtypeStruct((token_rows, width), BF16),
-            jax.ShapeDtypeStruct((token_rows, width), BF16),
-            jax.ShapeDtypeStruct((rows, part), F32),
+            jax.ShapeDtypeStruct((groups, segment, width * parts), BF16),
+            jax.ShapeDtypeStruct((groups * WINDOW, part), F32),
         ],
         scratch_shapes=[
+            pltpu.VMEM((parts, groups, WINDOW, part), BF16),
             pltpu.VMEM((2, WINDOW, width), BF16),
             pltpu.VMEM((2, WINDOW, width), BF16),
+            pltpu.VMEM((2, SPAN, width), BF16),
+            pltpu.VMEM((2, 16, width), BF16),
+            pltpu.VMEM((SPAN, width), F32),
+            pltpu.VMEM((SPAN, width), F32),
+            pltpu.VMEM((2, 16, width), BF16),
+            pltpu.VMEM((2, 16, width), BF16),
+            pltpu.VMEM((groups, parts, segment, width), BF16),
+            pltpu.VMEM((parts, groups, segment, width), BF16),
             pltpu.VMEM((groups, 2, chips, WINDOW, part), F32),
             pltpu.VMEM((groups, chips, WINDOW, part), F32),
             pltpu.VMEM((groups, chips - 1, WINDOW, part), F32),
             pltpu.VMEM((groups, chips - 1, WINDOW, part), F32),
-            pltpu.SemaphoreType.DMA((groups,)),
-            pltpu.SemaphoreType.DMA((groups,)),
-            pltpu.SemaphoreType.DMA((groups, chips - 1)),
-            pltpu.SemaphoreType.DMA((groups, chips - 1)),
+            dma((groups,)),
+            dma((groups,)),
+            dma((groups, chips - 1)),
+            dma((groups, chips - 1)),
+            dma((groups, chips - 1)),
+            dma((groups, chips - 1)),
+            dma((1,)),
+            dma((1,)),
+            dma((groups, parts - 1)),
+            dma((groups, parts - 1)),
+            dma((groups,)),
+            dma((groups,)),
+            dma((groups, chips - 1)),
+            dma((groups, chips - 1)),
         ],
         compiler_params=pltpu.CompilerParams(
             collective_id=1, has_side_effects=True, vmem_limit_bytes=48 << 20
         ),
-    )(features, kv_weight, query_rows, grad_rows)
+    )(picked, kv_weight, queries, grad_out, edge)
 
 
 def per_device(queries, encodings, kv_weight, grad_out, neighbour_owner, neighbour_slot):
     seq_count = lax.axis_size("seq")
     seq_index = lax.axis_index("seq")
+    parts = lax.axis_size("head")
     token_rows, width = queries.shape
     requests = token_rows // SPAN * NEIGHBOURS
     tile_rows, _, part = encodings.shape
-    forward = [(i, (i + 1) % seq_count) for i in range(seq_count)]
-    backward = [((i + 1) % seq_count, i) for i in range(seq_count)]
-
-    tile = neighbour_owner * tile_rows + neighbour_slot
-    tile = jnp.roll(tile, 1, axis=0).reshape(seq_count, requests)
-    tile = lax.dynamic_index_in_dim(tile, seq_index, 0, keepdims=False)
-
-    stored = gather_tiles(encodings, seq_count).reshape(-1, NEIGHBOUR_LEN, part)
-    picked = stored[tile].reshape(requests * NEIGHBOUR_LEN, part)
-    features = lax.all_gather(picked, "head", axis=0, tiled=False)
-
-    edge = jnp.stack([queries[-1:], grad_out[-1:]], 0)
-    edge = lax.ppermute(edge, "seq", forward)
-    row = lax.broadcasted_iota(jnp.int32, (token_rows, 1), 0)
-    unattending = (seq_index == 0) & (row >= 1) & (row < SPAN)
-    zero = jnp.zeros((), BF16)
-
-    def shifted(rows, first):
-        rows = jnp.concatenate([first, rows[:-1]], 0)
-        return jnp.where(unattending, zero, rows)
-
-    query_rows = shifted(queries, edge[0])
-    grad_rows = shifted(grad_out, edge[1])
-    att, qgrad, mine = run_groups(features, kv_weight, query_rows, grad_rows)
-
-    att = jnp.where(unattending, zero, att)
-    last = lax.ppermute(jnp.stack([att[:1], qgrad[:1]], 0), "seq", backward)
-    attended = jnp.concatenate([att[1:], last[0]], 0)
-    qgrad = jnp.concatenate([qgrad[1:], last[1]], 0).reshape(-1, SPAN, width)
-    query_grad = lax.all_to_all(qgrad, "head", split_axis=1, concat_axis=2, tiled=True)
-
+
+    pick = jnp.stack([neighbour_owner, neighbour_slot], 0)
+    pick = jnp.roll(pick, 1, axis=1).reshape(2, seq_count, requests)
+    pick = lax.dynamic_index_in_dim(pick, seq_index, 1, keepdims=False)
+    edge = jnp.stack([queries[-16:], grad_out[-16:]], 0)
+    picked, edge = gather_tiles(pick, encodings, edge, seq_count)
+    picked = picked.reshape(requests // NEIGHBOURS, WINDOW, part)
+    attended, query_grad, mine = run_groups(
+        picked, kv_weight, queries, grad_out, edge, parts, seq_count
+    )
     mine = mine.reshape(requests, NEIGHBOUR_LEN, part)
+    tile = pick[0] * tile_rows + pick[1]
     share = (jnp.arange(seq_count * tile_rows)[:, None] == tile[None, :]).astype(F32)
     total = scatter_tiles(share, mine, seq_count, tile_rows)
     return attended, query_grad, total

time: 156 us -> 123 us (0.79)
  waiting for transfers between devices: 22.3 us -> 0 us
  Pallas kernels: 100 us -> 114 us
  between operations: 14.2 us -> 0.7 us
  starting transfers between devices: 8.83 us -> 0 us
  local copies, waits for them, and re-layouts: 7.9 us -> 6.23 us
    all_gather x1 -> x0, waiting for transfers between devices: 15.7 us -> none  [per_device(): features = lax.all_gather(picked, 'head', axis=0, tiled=False)]
    pallas_call x1, Pallas kernels: 41.1 us -> 53.6 us  [run_groups(): pl.pallas_call(functools.partial(group_body, parts, count), in_specs=[vme...]
    ppermute x2 -> x0, waiting for transfers between devices: 6.6 us -> none  [the longest x1 5.36 us: per_device(): edge = lax.ppermute(edge, 'seq', forward)]
    ppermute x2 -> x0, starting transfers between devices: 5.32 us -> none  [the longest x1 4.29 us: per_device(): last = lax.ppermute(jnp.stack([att[:1], qgrad[:1]], 0), 'seq', backward)]
    all_to_all x1 -> x0, starting transfers between devices: 3.47 us -> none  [per_device(): lax.all_to_all(qgrad, 'head', split_axis=1, concat_axis=2, tiled=True)]
    pallas_call x1, Pallas kernels: 23.2 us -> 25.7 us  [gather_tiles(): pl.pallas_call(functools.partial(gather_body, count), in_specs=[pl.BlockS...]
    unnamed x9, local copies, waits for them, and re-layouts: 3.2 us -> 5.26 us
    all_to_all x2 -> x0, local copies, waits for them, and re-layouts: 1.58 us -> none  [per_device(): lax.all_to_all(qgrad, 'head', split_axis=1, concat_axis=2, tiled=True)]
  transfers between devices with their start and end apart: 4 -> 0, of which waited for: 3 -> 0; matrix products, arithmetic and copies ran while one was open for 1% -> 0% of each run, Pallas kernels for 23% -> 0%
where the time goes in v3:
time: 123 us
  Pallas kernels  114 us (93%)
  local copies, waits for them, and re-layouts  6.23 us (5%)
  other arithmetic  1.57 us (1%)
    pallas_call x1, Pallas kernels, run_groups(): pl.pallas_call(functools.partial(group_body, parts, count), in_specs=[vme...  53.6 us
    pallas_call x1, Pallas kernels, scatter_tiles(): pl.pallas_call(functools.partial(scatter_body, count), in_specs=[pl.Block...  35 us
    pallas_call x1, Pallas kernels, gather_tiles(): pl.pallas_call(functools.partial(gather_body, count), in_specs=[pl.BlockS...  25.7 us
    unnamed x9, local copies, waits for them, and re-layouts  5.26 us

profile of v3, /device:TPU:0, one launch (start us, length us, event | category | flops | bytes accessed | tf_op | source)
XLA Modules:
  0.0 122.9 jit_solution(4213057449656665077)
XLA Ops:
  0.6 0.7 pad_add_fusion
  1.3 0.8 slice_add_fusion
  2.1 0.1 pad_add_fusion.1
  2.2 0.1 copy.10
  2.3 0.1 reshape.32
  2.4 0.8 slice_bitcast_fusion
  3.2 0.0 copy-start.2
  3.2 0.9 copy-done.2
  4.1 25.7 %shard_map.85 = (bf16[8,128,256]{2,1,0:T(8,128)(2,1)S(1)}, bf16[2,16,1024]{2,1,0:T(8,128)(2,1)S(1)}) custom-call(s32[2,8]{1,0:T(2,128)S(1)} %bitcast.13, bf16[3,128,256]{2,1,0:T(8,128)(2,1)S(1)} %copy-done.2, bf16[2,16,1024]{2,1,0:T(8,128)(2,1)S(1)} %pad_maximum_fusion.edge_ref), custom_call_target="tpu_custom_call" | custom-call | tf_op jit(solution)/shard_map/pallas_call | solution.py:98
  29.8 0.0 copy-start
  29.9 1.0 copy-done
  30.9 0.0 copy-start.1
  30.9 1.0 copy-done.1
  31.9 53.6 %shard_map.86 = (bf16[256,1024]{1,0:T(8,128)(2,1)S(1)}, bf16[4,16,4096]{2,1,0:T(8,128)(2,1)S(1)}, f32[1024,256]{1,0:T(8,128)S(1)}) custom-call(bf16[4,256,256]{2,1,0:T(8,128)(2,1)S(1)} %bitcast.12, bf16[2,1024,1024]{2,1,0:T(8,128)(2,1)} %weight_ref.1, bf16[256,1024]{1,0:T(8,128)(2,1)S(1)} %copy-done.1, bf16[256,1024]{1,0:T(8,128)(2,1)S(1)} %copy-done, ...), custom_call_target="tpu_custom_call" | custom-call | tf_op jit(solution)/shard_map/pallas_call | solution.py:405
  85.6 35.0 %shard_map.87 = bf16[3,128,256]{2,1,0:T(8,128)(2,1)S(1)} custom-call(f32[24,8]{1,0:T(8,128)S(1)} %fusion.share_ref, f32[8,128,256]{2,1,0:T(8,128)S(1)} %bitcast.11), custom_call_target="tpu_custom_call" | custom-call | tf_op jit(solution)/shard_map/pallas_call | solution.py:182
  120.6 0.8 copy.14
  121.4 0.8 copy.15
  122.2 0.7 copy.16
  (4 shorter events, 0.0 us)
Async XLA Ops:
  3.2 0.9 copy-start.2
  29.8 1.0 copy-start
  30.9 1.0 copy-start.1

commit v4 on v3

--- a/solution.py
+++ b/solution.py
@@ -53,7 +53,8 @@
 
 
 def gather_body(
-    count, pick_ref, shard_ref, edge_ref, picked_ref, edge_out, stored, send, recv, edge_send, edge_recv
+    count, pick_ref, shard_ref, query_ref, grad_ref, picked_ref, edge_out, stored,
+    send, recv, edge_send, edge_recv,
 ):
     me = lax.axis_index("seq")
     place = ring_place(me, count)
@@ -73,7 +74,11 @@
         )
 
     lanes = [(way, half) for half in range(2) for way in range(2)]
-    edge = remote(edge_ref, edge_out, edge_send.at[0], edge_recv.at[0], "seq", after)
+    ending = pl.ds(query_ref.shape[0] - 16, 16)
+    edges = [
+        remote(ref.at[ending, :], edge_out.at[c], edge_send.at[c], edge_recv.at[c], "seq", after)
+        for c, ref in ((0, query_ref), (1, grad_ref))
+    ]
     for step in range(count // 2):
         for way, half in lanes:
             if step < hops[way][half]:
@@ -81,46 +86,54 @@
                     copy(way, half, step - 1).wait_recv()
                 copy(way, half, step).start()
         if step == 0:
-            edge.start()
+            for edge in edges:
+                edge.start()
     for way, half in lanes:
         copy(way, half, hops[way][half] - 1).wait_recv()
     for r in range(picked_ref.shape[0]):
         picked_ref[r] = stored[pick_ref[0, r], pick_ref[1, r]]
-    edge.wait()
+    for edge in edges:
+        edge.wait()
     for way, half in lanes:
         for step in range(hops[way][half]):
             copy(way, half, step).wait_send()
 
 
-def gather_tiles(pick, shard, edge, count):
+def gather_tiles(pick, shard, queries, grad_out, count):
     tiles, rows, part = shard.shape
     vmem = pl.BlockSpec(memory_space=pltpu.VMEM)
     return pl.pallas_call(
         functools.partial(gather_body, count),
-        in_specs=[pl.BlockSpec(memory_space=pltpu.SMEM), vmem, vmem],
+        in_specs=[pl.BlockSpec(memory_space=pltpu.SMEM), vmem]
+        + [pl.BlockSpec(memory_space=pl.ANY)] * 2,
         out_specs=[vmem, vmem],
         out_shape=[
             jax.ShapeDtypeStruct((pick.shape[1], rows, part), shard.dtype),
-            jax.ShapeDtypeStruct(edge.shape, edge.dtype),
+            jax.ShapeDtypeStruct((2, 16, queries.shape[1]), queries.dtype),
         ],
         scratch_shapes=[
             pltpu.VMEM((count, tiles, rows, part), shard.dtype),
             pltpu.SemaphoreType.DMA((2, 2, count // 2)),
             pltpu.SemaphoreType.DMA((2, 2, count // 2)),
-            pltpu.SemaphoreType.DMA((1,)),
-            pltpu.SemaphoreType.DMA((1,)),
+            pltpu.SemaphoreType.DMA((2,)),
+            pltpu.SemaphoreType.DMA((2,)),
         ],
         compiler_params=pltpu.CompilerParams(
             collective_id=0, has_side_effects=True, vmem_limit_bytes=32 << 20
         ),
-    )(pick, shard, edge)
-
-
-def scatter_body(count, share_ref, mine_ref, out_ref, buf, send, recv):
+    )(pick, shard, queries, grad_out)
+
+
+def scatter_body(
+    count, share_ref, mine_ref, qout, out_ref, qgrad_ref, buf, qin, send, recv, q_send, q_recv
+):
+    head = lax.axis_index("head")
+    groups, parts, _, width = qout.shape
+    others = [(head + d) % parts for d in range(1, parts)]
     me = lax.axis_index("seq")
     place = ring_place(me, count)
     neighbours = (ring_index(place + 1, count), ring_index(place - 1, count))
-    meet([("seq", other) for other in neighbours])
+    meet([("seq", other) for other in neighbours] + [("head", other) for other in others])
     tiles, length, _ = out_ref.shape
     requests = mine_ref.shape[0]
     rows = length // 2
@@ -145,10 +158,25 @@
             neighbours[way],
         )
 
+    def to_head(i, d):
+        return remote(
+            qout.at[i, others[d - 1]],
+            qin.at[head, i],
+            q_send.at[i, d - 1],
+            q_recv.at[i, d - 1],
+            "head",
+            others[d - 1],
+        )
+
     for k in range(tiles):
         for way in range(2):
             buf[way, 0, k] = own(way, target_of(way, 0), k)
             copy(way, 0, k).start()
+
+    for i in range(groups):
+        for d in range(1, parts):
+            to_head(i, d).start()
+        qgrad_ref[i, :, pl.ds(pl.multiple_of(head * width, width), width)] = qout[i, head]
 
     def step_body(step, carry):
         for k in range(tiles):
@@ -160,6 +188,12 @@
         return carry
 
     lax.fori_loop(1, count - 1, step_body, 0)
+    for i in range(groups):
+        for d in range(1, parts):
+            source = (head + parts - d) % parts
+            to_head(i, d).wait_recv()
+            columns = pl.ds(pl.multiple_of(source * width, width), width)
+            qgrad_ref[i, :, columns] = qin[source, i]
     for k in range(tiles):
         for way in range(2):
             piece = own(way, me, k)
@@ -175,36 +209,48 @@
         return carry
 
     lax.fori_loop(0, count - 1, drain, 0)
-
-
-def scatter_tiles(share, mine, count, tiles):
+    for i in range(groups):
+        for d in range(1, parts):
+            to_head(i, d).wait_send()
+
+
+def scatter_tiles(share, mine, qout, count, tiles):
     _, length, part = mine.shape
+    groups, parts, segment, width = qout.shape
+    vmem = pl.BlockSpec(memory_space=pltpu.VMEM)
     return pl.pallas_call(
         functools.partial(scatter_body, count),
         in_specs=[
             pl.BlockSpec(memory_space=pltpu.SMEM),
-            pl.BlockSpec(memory_space=pltpu.VMEM),
-        ],
-        out_specs=pl.BlockSpec(memory_space=pltpu.VMEM),
-        out_shape=jax.ShapeDtypeStruct((tiles, length, part), BF16),
+            vmem,
+            vmem,
+        ],
+        out_specs=[vmem, vmem],
+        out_shape=[
+            jax.ShapeDtypeStruct((tiles, length, part), BF16),
+            jax.ShapeDtypeStruct((groups, segment, parts * width), BF16),
+        ],
         scratch_shapes=[
             pltpu.VMEM((2, count, tiles, length // 2, part), F32),
+            pltpu.VMEM((parts, groups, segment, width), BF16),
             pltpu.SemaphoreType.DMA((2, count - 1, tiles)),
             pltpu.SemaphoreType.DMA((2, count - 1, tiles)),
+            pltpu.SemaphoreType.DMA((groups, parts - 1)),
+            pltpu.SemaphoreType.DMA((groups, parts - 1)),
         ],
         compiler_params=pltpu.CompilerParams(
             collective_id=2, has_side_effects=True, vmem_limit_bytes=32 << 20
         ),
-    )(share, mine)
+    )(share, mine, qout)
 
 
 def group_body(
     parts, count, picked_ref, weight_ref, query_ref, grad_ref, edge_ref,
-    att_ref, qgrad_ref, out_ref,
-    feat, kv, kv_grad, rows_in, tail, att_rows, qgrad_rows, edge_out, edge_in, qout, qin,
+    att_ref, qout, out_ref,
+    feat, kv, kv_grad, rows_in, tail, att_rows, qgrad_rows, edge_out, edge_in,
     term, from_core, across, from_chip,
     pick_send, pick_recv, far_send, far_recv, pass_send, pass_recv,
-    edge_send, edge_recv, q_send, q_recv, core_send, core_recv, chip_send, chip_recv,
+    edge_send, edge_recv, core_send, core_recv, chip_send, chip_recv,
 ):
     head = lax.axis_index("head")
     seq = lax.axis_index("seq")
@@ -212,10 +258,9 @@
     chips = parts // 2
     sibling = chip * 2 + 1 - core
     peers = [((chip + d) % chips) * 2 + core for d in range(1, chips)]
-    others = [(head + d) % parts for d in range(1, parts)]
     before = (seq + count - 1) % count
     after = (seq + 1) % count
-    meet([("head", other) for other in others] + [("seq", before), ("seq", after)])
+    meet([("head", other) for other in [sibling] + peers] + [("seq", before), ("seq", after)])
     part = picked_ref.shape[2]
     width = query_ref.shape[1]
     groups = query_ref.shape[0] // SPAN
@@ -247,9 +292,15 @@
             to_far(i, d).wait_recv()
             pass_far(i, d).start()
 
-    def to_core(i):
-        return remote(
-            term.at[i, 1 - core], from_core.at[i], core_send.at[i], core_recv.at[i], "head", sibling
+    def to_core(i, d):
+        target = (chip + d) % chips
+        return remote(
+            term.at[i, 1 - core, target],
+            from_core.at[i, target],
+            core_send.at[i, d],
+            core_recv.at[i, d],
+            "head",
+            sibling,
         )
 
     def to_chip(i, d):
@@ -262,22 +313,12 @@
             peers[d - 1],
         )
 
-    def to_head(i, d):
-        return remote(
-            qout.at[i, others[d - 1]],
-            qin.at[head, i],
-            q_send.at[i, d - 1],
-            q_recv.at[i, d - 1],
-            "head",
-            others[d - 1],
-        )
-
     edge = remote(edge_out, edge_in, edge_send.at[0], edge_recv.at[0], "seq", before)
 
     def pass_on(i):
-        to_core(i).wait_recv()
         for d in range(1, chips):
             target = (chip + d) % chips
+            to_core(i, d).wait_recv()
             across[i, d - 1] = term[i, core, target] + from_core[i, target]
             to_chip(i, d).start()
 
@@ -291,9 +332,6 @@
         qout[i, parts - 1] = jnp.where(
             last_segment, qgrad16[16 - segment :], qout[i, parts - 1].astype(F32)
         ).astype(BF16)
-        qin[head, i] = qout[i, head]
-        for d in range(1, parts):
-            to_head(i, d).start()
 
     for i in range(groups):
         for d in range(1, chips):
@@ -344,12 +382,16 @@
             qgrad_rows[:, cols] = dot(dscore, k, 1, 0) * SCALE
             kv_grad[0, :, cols] = (dot(dscore, q, 0, 0) * SCALE).astype(BF16)
             kv_grad[1, :, cols] = dot(half, g, 0, 0).astype(BF16)
-        for j in range(parts):
-            rows = slice(j * part, (j + 1) * part)
-            term[i, j % 2, j // 2] = dot(kv_grad[0], weight_ref[0, rows, :], 1, 1) + dot(
-                kv_grad[1], weight_ref[1, rows, :], 1, 1
-            )
-        to_core(i).start()
+        for d in [*range(1, chips), 0]:
+            target = (chip + d) % chips
+            for c in (1 - core, core):
+                first = (target * 2 + c) * part
+                rows = pl.ds(pl.multiple_of(first, part), part)
+                term[i, c, target] = dot(kv_grad[0], weight_ref[0, rows, :], 1, 1) + dot(
+                    kv_grad[1], weight_ref[1, rows, :], 1, 1
+                )
+                if c is not core:
+                    to_core(i, d).start()
         att = jnp.where(place >= limit, att_rows[...], 0.0)
         att_ref[tokens, :] = att.astype(BF16)
         for j in range(parts):
@@ -363,16 +405,16 @@
 
         @pl.when(i > 0)
         def _():
-            pass_on(i - 1)
             finish_span(i - 1, att_rows[SPAN - 16 :, :], qgrad_rows[SPAN - 16 :, :])
 
+        pass_on(i)
         return carry
 
     lax.fori_loop(0, groups, group, 0)
-    pass_on(groups - 1)
     edge.wait_recv()
     finish_span(groups - 1, edge_in[0].astype(F32), edge_in[1].astype(F32))
     for i in range(groups):
+        to_core(i, 0).wait_recv()
         total = term[i, core, chip] + from_core[i, chip]
         for d in range(1, chips):
             to_chip(i, d).wait_recv()
@@ -380,19 +422,13 @@
         out_ref[i * WINDOW : (i + 1) * WINDOW, :] = total
     edge.wait_send()
     for i in range(groups):
-        for d in range(1, parts):
-            to_head(i, d).wait_recv()
-        for j in range(parts):
-            qgrad_ref[i, :, j * width : (j + 1) * width] = qin[j, i]
-    for i in range(groups):
-        to_core(i).wait_send()
+        for d in range(chips):
+            to_core(i, d).wait_send()
         to_sibling(i).wait_send()
         for d in range(1, chips):
             to_chip(i, d).wait_send()
             to_far(i, d).wait_send()
             pass_far(i, d).wait_send()
-        for d in range(1, parts):
-            to_head(i, d).wait_send()
 
 
 def run_groups(picked, kv_weight, queries, grad_out, edge, parts, count):
@@ -408,7 +444,7 @@
         out_specs=[vmem] * 3,
         out_shape=[
             jax.ShapeDtypeStruct((token_rows, width), BF16),
-            jax.ShapeDtypeStruct((groups, segment, width * parts), BF16),
+            jax.ShapeDtypeStruct((groups, parts, segment, width), BF16),
             jax.ShapeDtypeStruct((groups * WINDOW, part), F32),
         ],
         scratch_shapes=[
@@ -421,8 +457,6 @@
             pltpu.VMEM((SPAN, width), F32),
             pltpu.VMEM((2, 16, width), BF16),
             pltpu.VMEM((2, 16, width), BF16),
-            pltpu.VMEM((groups, parts, segment, width), BF16),
-            pltpu.VMEM((parts, groups, segment, width), BF16),
             pltpu.VMEM((groups, 2, chips, WINDOW, part), F32),
             pltpu.VMEM((groups, chips, WINDOW, part), F32),
             pltpu.VMEM((groups, chips - 1, WINDOW, part), F32),
@@ -435,10 +469,8 @@
             dma((groups, chips - 1)),
             dma((1,)),
             dma((1,)),
-            dma((groups, parts - 1)),
-            dma((groups, parts - 1)),
-            dma((groups,)),
-            dma((groups,)),
+            dma((groups, chips)),
+            dma((groups, chips)),
             dma((groups, chips - 1)),
             dma((groups, chips - 1)),
         ],
@@ -459,16 +491,15 @@
     pick = jnp.stack([neighbour_owner, neighbour_slot], 0)
     pick = jnp.roll(pick, 1, axis=1).reshape(2, seq_count, requests)
     pick = lax.dynamic_index_in_dim(pick, seq_index, 1, keepdims=False)
-    edge = jnp.stack([queries[-16:], grad_out[-16:]], 0)
-    picked, edge = gather_tiles(pick, encodings, edge, seq_count)
+    picked, edge = gather_tiles(pick, encodings, queries, grad_out, seq_count)
     picked = picked.reshape(requests // NEIGHBOURS, WINDOW, part)
-    attended, query_grad, mine = run_groups(
+    attended, qout, mine = run_groups(
         picked, kv_weight, queries, grad_out, edge, parts, seq_count
     )
     mine = mine.reshape(requests, NEIGHBOUR_LEN, part)
     tile = pick[0] * tile_rows + pick[1]
     share = (jnp.arange(seq_count * tile_rows)[:, None] == tile[None, :]).astype(F32)
-    total = scatter_tiles(share, mine, seq_count, tile_rows)
+    total, query_grad = scatter_tiles(share, mine, qout, seq_count, tile_rows)
     return attended, query_grad, total
 
 

time: 123 us -> 119 us (0.967)
  Pallas kernels: 114 us -> 109 us
  local copies, waits for them, and re-layouts: 6.23 us -> 7.53 us
    pallas_call x1, Pallas kernels: 53.6 us -> 48.2 us  [run_groups(): pl.pallas_call(functools.partial(group_body, parts, count), in_specs=[vme...]
    unnamed x9 -> x13, local copies, waits for them, and re-layouts: 5.26 us -> 7.35 us
where the time goes in v4:
time: 119 us
  Pallas kernels  109 us (92%)
  local copies, waits for them, and re-layouts  7.53 us (6%)
  other arithmetic  1.56 us (1%)
    pallas_call x1, Pallas kernels, run_groups(): pl.pallas_call(functools.partial(group_body, parts, count), in_specs=[vme...  48.2 us
    pallas_call x1, Pallas kernels, scatter_tiles(): pl.pallas_call(functools.partial(scatter_body, count), in_specs=[pl.Block...  35.3 us
    pallas_call x1, Pallas kernels, gather_tiles(): pl.pallas_call(functools.partial(gather_body, count), in_specs=[pl.BlockS...  25.8 us
    unnamed x13, local copies, waits for them, and re-layouts  7.35 us

profile of v4, /device:TPU:0, one launch (start us, length us, event | category | flops | bytes accessed | tf_op | source)
XLA Modules:
  0.0 119.1 jit_solution(2186262105452267009)
XLA Ops:
  0.6 0.7 pad_add_fusion
  1.3 0.8 slice_add_fusion
  2.1 0.1 pad_add_fusion.1
  2.2 0.1 copy.10
  2.3 0.1 reshape.32
  2.4 0.0 copy-start
  2.4 1.0 copy-done
  3.4 0.0 copy-start.2
  3.4 1.0 copy-done.2
  4.5 0.0 copy-start.4
  4.5 0.9 copy-done.4
  5.4 25.8 %shard_map.85 = (bf16[8,128,256]{2,1,0:T(8,128)(2,1)S(1)}, bf16[2,16,1024]{2,1,0:T(8,128)(2,1)S(1)}) custom-call(s32[2,8]{1,0:T(2,128)S(1)} %bitcast.9, bf16[3,128,256]{2,1,0:T(8,128)(2,1)S(1)} %copy-done.4, bf16[256,1024]{1,0:T(8,128)(2,1)S(1)} %copy-done, bf16[256,1024]{1,0:T(8,128)(2,1)S(1)} %copy-done.2), custom_call_target="tpu_custom_call" | custom-call | tf_op jit(solution)/shard_map/pallas_call | solution.py:105
  31.2 0.0 copy-start.1
  31.2 1.0 copy-done.1
  32.2 0.0 copy-start.3
  32.2 1.0 copy-done.3
  33.3 48.2 %shard_map.86 = (bf16[256,1024]{1,0:T(8,128)(2,1)S(1)}, bf16[4,4,16,1024]{3,2,1,0:T(8,128)(2,1)S(1)}, f32[1024,256]{1,0:T(8,128)S(1)}) custom-call(bf16[4,256,256]{2,1,0:T(8,128)(2,1)S(1)} %bitcast.8, bf16[2,1024,1024]{2,1,0:T(8,128)(2,1)} %weight_ref.1, bf16[256,1024]{1,0:T(8,128)(2,1)S(1)} %copy-done.1, bf16[256,1024]{1,0:T(8,128)(2,1)S(1)} %copy-done.3, ...), custom_call_target="tpu_custom_call" | custom-call | tf_op jit(solution)/shard_map/pallas_call | solution.py:441
  81.5 35.3 %shard_map.87 = (bf16[3,128,256]{2,1,0:T(8,128)(2,1)S(1)}, bf16[4,16,4096]{2,1,0:T(8,128)(2,1)S(1)}) custom-call(f32[24,8]{1,0:T(8,128)S(1)} %fusion.share_ref, f32[8,128,256]{2,1,0:T(8,128)S(1)} %bitcast.7, bf16[4,4,16,1024]{3,2,1,0:T(8,128)(2,1)S(1)} %get-tuple-element.14.qout), custom_call_target="tpu_custom_call" | custom-call | tf_op jit(solution)/shard_map/pallas_call | solution.py:221
  116.8 0.8 copy.14
  117.6 0.8 copy.15
  118.4 0.7 copy.16
  (3 shorter events, 0.0 us)
Async XLA Ops:
  2.4 1.0 copy-start
  3.4 1.0 copy-start.2
  4.5 0.9 copy-start.4
  31.2 1.0 copy-start.1
  32.2 1.0 copy-start.3

commit v5 on v4

--- a/solution.py
+++ b/solution.py
@@ -105,7 +105,7 @@
     return pl.pallas_call(
         functools.partial(gather_body, count),
         in_specs=[pl.BlockSpec(memory_space=pltpu.SMEM), vmem]
-        + [pl.BlockSpec(memory_space=pl.ANY)] * 2,
+        + [pl.BlockSpec(memory_space=pltpu.HBM)] * 2,
         out_specs=[vmem, vmem],
         out_shape=[
             jax.ShapeDtypeStruct((pick.shape[1], rows, part), shard.dtype),
@@ -245,15 +245,21 @@
 
 
 def group_body(
-    parts, count, picked_ref, weight_ref, query_ref, grad_ref, edge_ref,
+    parts, count, picked_ref, weight_ref, query_hbm, grad_hbm, edge_ref,
     att_ref, qout, out_ref,
-    feat, kv, kv_grad, rows_in, tail, att_rows, qgrad_rows, edge_out, edge_in,
+    query_ref, grad_ref, load_sem, feat, kv, kv_grad, rows_in, tail, att_rows, qgrad_rows, edge_out, edge_in,
     term, from_core, across, from_chip,
     pick_send, pick_recv, far_send, far_recv, pass_send, pass_recv,
     edge_send, edge_recv, core_send, core_recv, chip_send, chip_recv,
 ):
     head = lax.axis_index("head")
     seq = lax.axis_index("seq")
+    loads = [
+        pltpu.make_async_copy(query_hbm, query_ref, load_sem.at[0]),
+        pltpu.make_async_copy(grad_hbm, grad_ref, load_sem.at[1]),
+    ]
+    for load in loads:
+        load.start()
     core, chip = head % 2, head // 2
     chips = parts // 2
     sibling = chip * 2 + 1 - core
@@ -340,6 +346,8 @@
     for i in range(groups):
         feat[head, i] = picked_ref[i]
     tail[...] = edge_ref[...]
+    for load in loads:
+        load.wait()
     hand_over(0)
 
     def group(i, carry):
@@ -437,10 +445,11 @@
     chips = parts // 2
     segment = SPAN // parts
     vmem = pl.BlockSpec(memory_space=pltpu.VMEM)
+    hbm = pl.BlockSpec(memory_space=pltpu.HBM)
     dma = pltpu.SemaphoreType.DMA
     return pl.pallas_call(
         functools.partial(group_body, parts, count),
-        in_specs=[vmem] * 5,
+        in_specs=[vmem, vmem, hbm, hbm, vmem],
         out_specs=[vmem] * 3,
         out_shape=[
             jax.ShapeDtypeStruct((token_rows, width), BF16),
@@ -448,6 +457,9 @@
             jax.ShapeDtypeStruct((groups * WINDOW, part), F32),
         ],
         scratch_shapes=[
+            pltpu.VMEM((token_rows, width), BF16),
+            pltpu.VMEM((token_rows, width), BF16),
+            dma((2,)),
             pltpu.VMEM((parts, groups, WINDOW, part), BF16),
             pltpu.VMEM((2, WINDOW, width), BF16),
             pltpu.VMEM((2, WINDOW, width), BF16),
@@ -491,6 +503,8 @@
     pick = jnp.stack([neighbour_owner, neighbour_slot], 0)
     pick = jnp.roll(pick, 1, axis=1).reshape(2, seq_count, requests)
     pick = lax.dynamic_index_in_dim(pick, seq_index, 1, keepdims=False)
+    queries = pltpu.with_memory_space_constraint(queries, pltpu.HBM)
+    grad_out = pltpu.with_memory_space_constraint(grad_out, pltpu.HBM)
     picked, edge = gather_tiles(pick, encodings, queries, grad_out, seq_count)
     picked = picked.reshape(requests // NEIGHBOURS, WINDOW, part)
     attended, qout, mine = run_groups(

time: 119 us -> 115 us (0.966)
  local copies, waits for them, and re-layouts: 7.53 us -> 3.37 us
    unnamed x13 -> x5, local copies, waits for them, and re-layouts: 7.35 us -> 3.19 us
where the time goes in v5:
time: 115 us
  Pallas kernels  109 us (95%)
  local copies, waits for them, and re-layouts  3.37 us (3%)
  other arithmetic  1.56 us (1%)
    pallas_call x1, Pallas kernels, run_groups(): pl.pallas_call(functools.partial(group_body, parts, count), in_specs=[vme...  48.3 us
    pallas_call x1, Pallas kernels, scatter_tiles(): pl.pallas_call(functools.partial(scatter_body, count), in_specs=[pl.Block...  35.3 us
    pallas_call x1, Pallas kernels, gather_tiles(): pl.pallas_call(functools.partial(gather_body, count), in_specs=[pl.BlockS...  25.8 us
    unnamed x5, local copies, waits for them, and re-layouts  3.19 us

profile of v5, /device:TPU:0, one launch (start us, length us, event | category | flops | bytes accessed | tf_op | source)
XLA Modules:
  0.0 114.9 jit_solution(3875395277255013489)
XLA Ops:
  0.6 0.7 pad_add_fusion
  1.3 0.8 slice_add_fusion
  2.1 0.1 pad_add_fusion.1
  2.2 0.1 copy.10
  2.3 0.1 reshape.32
  2.4 0.0 copy-start
  2.4 0.9 copy-done
  3.3 25.8 %shard_map.85 = (bf16[8,128,256]{2,1,0:T(8,128)(2,1)S(1)}, bf16[2,16,1024]{2,1,0:T(8,128)(2,1)S(1)}) custom-call(s32[2,8]{1,0:T(2,128)S(1)} %bitcast.9, bf16[3,128,256]{2,1,0:T(8,128)(2,1)S(1)} %copy-done, bf16[256,1024]{1,0:T(8,128)(2,1)} %query_hbm.1, bf16[256,1024]{1,0:T(8,128)(2,1)} %grad_hbm.1), custom_call_target="tpu_custom_call" | custom-call | tf_op jit(solution)/shard_map/pallas_call | solution.py:105
  29.1 48.3 %shard_map.86 = (bf16[256,1024]{1,0:T(8,128)(2,1)S(1)}, bf16[4,4,16,1024]{3,2,1,0:T(8,128)(2,1)S(1)}, f32[1024,256]{1,0:T(8,128)S(1)}) custom-call(bf16[4,256,256]{2,1,0:T(8,128)(2,1)S(1)} %bitcast.8, bf16[2,1024,1024]{2,1,0:T(8,128)(2,1)} %weight_ref.1, bf16[256,1024]{1,0:T(8,128)(2,1)} %query_hbm.1, bf16[256,1024]{1,0:T(8,128)(2,1)} %grad_hbm.1, ...), custom_call_target="tpu_custom_call" | custom-call | tf_op jit(solution)/shard_map/pallas_call | solution.py:450
  77.4 35.3 %shard_map.87 = (bf16[3,128,256]{2,1,0:T(8,128)(2,1)S(1)}, bf16[4,16,4096]{2,1,0:T(8,128)(2,1)S(1)}) custom-call(f32[24,8]{1,0:T(8,128)S(1)} %fusion.share_ref, f32[8,128,256]{2,1,0:T(8,128)S(1)} %bitcast.7, bf16[4,4,16,1024]{3,2,1,0:T(8,128)(2,1)S(1)} %get-tuple-element.14.qout), custom_call_target="tpu_custom_call" | custom-call | tf_op jit(solution)/shard_map/pallas_call | solution.py:221
  112.7 0.8 copy.14
  113.5 0.8 copy.15
  114.3 0.7 copy.16
  (3 shorter events, 0.0 us)
Async XLA Ops:
  2.4 0.9 copy-start
